TPU v7x, 32 devices: a whole 2x2x4 slice. The times are simulated.
32 devices in a mesh: col: 16 (over z, y, x), row: 2 (over core).
Axes of the slice: x: 2, y: 2, z: 4, core: 2. Of those that a mesh axis runs over, the one named last changes fastest.
Arguments:
- top_rows: float32 [1792, 8192], P(None, ('col', 'row')), may hold values from -0.0625 to 0.0625
- lower_new: float32 [8192, 256], P(('col', 'row')), may hold values from -6 to 6
- block_order: int32 [32, 2], P(('col', 'row')), may hold values from 0 to 1, each once within a row
- corner: float32 [1792, 1792], P('row'), may hold values from -0.125 to 0.125
- target: float32 [1792, 256], P('row'), may hold values from -6 to 6
- coupling: float32 [128, 128], replicated, may hold values from -0.5 to 0.5
- top_right: float32 [14, 128, 128], P('row'), may hold values from -0.5 to 0.5
- top_left: float32 [14, 128, 128], P('row'), may hold values from -0.5 to 0.5
- top_values: float32 [14, 128], P('row'), may hold values from 0.5 to 2
- new_right: float32 [2, 128, 128], replicated, may hold values from -0.5 to 0.5
- new_left: float32 [2, 128, 128], replicated, may hold values from -0.5 to 0.5
- new_values: float32 [2, 128], replicated, may hold values from 0.5 to 2
Outputs:
- solution: float32 [1792, 256], P('row')
Inputs may be any that keep to these rules, and one draw needn't show every extreme that they name: Each row of block_order is an ordering of 0 to 1.
All inputs are finite; a program needn't handle non-finite values.
Results may differ from a plain program's by a relative error of at most 0.0001.
Values sent between devices are 32-bit elements; how exact they have to be, the bound alone decides.
No kernel may reach another device: no remote copies, remote signals or barrier semaphores. Data moves between devices by JAX's collectives and lax.ppermute only.
A program may use at most 64 MiB of HBM per device.

v0:
```python
import functools

import jax
import jax.numpy as jnp
from jax import lax
from jax.experimental import pallas as pl
from jax.experimental.pallas import tpu as pltpu
from jax.sharding import PartitionSpec as P


F32 = jnp.float32
BF16 = jnp.bfloat16
GRANT = 12 << 20

VMEM = pl.BlockSpec(memory_space=pltpu.VMEM)
SMEM = pl.BlockSpec(memory_space=pltpu.SMEM)


def split(x):
    high = x.astype(BF16)
    return high, (x - high.astype(F32)).astype(BF16)


def mm(a, b):
    return jnp.dot(a, b, preferred_element_type=F32)


def cat(parts, axis):
    return jnp.concatenate(parts, axis=axis)


def lhs(x):
    return cat(split(x), 1)


def wide_rhs(x):
    high, low = split(x)
    return cat([high, high], 0), low


def wide_dot(a, b):
    n = a.shape[1] // 2
    return mm(a, b[0]) + mm(a[:, :n], b[1])


def block_rhs(x):
    both = cat(split(x), 1)
    return cat([both, both], 0)


def block_dot(a, b):
    n = b.shape[1] // 2
    r = mm(a, b)
    return r[:, :n] + r[:, n:]


def params(**kw):
    return pltpu.CompilerParams(vmem_limit_bytes=GRANT, **kw)


def partial_kernel(where, half, order, a_ref, b_ref, out_ref):
    slots, depth, _ = out_ref.shape
    size = b_ref.shape[0] // order.shape[1]
    paired = [
        b_ref[pl.ds(pl.multiple_of(order[0, g] * size, size), size), :]
        for g in range(order.shape[1])
    ]
    high, low = split(cat(paired, 0))
    for m in range(slots):
        rows = (half[0] * slots + (where[0] ^ m)) * depth
        ah, al = split(a_ref[pl.ds(pl.multiple_of(rows, 8), depth), :])
        out_ref[m] = mm(ah, high) + (mm(ah, low) + mm(al, high))


def partial_product(where, half, order, top_rows, lower, slots):
    depth = top_rows.shape[0] // 2 // slots
    return pl.pallas_call(
        partial_kernel,
        out_shape=jax.ShapeDtypeStruct((slots, depth, lower.shape[1]), F32),
        in_specs=[SMEM, SMEM, SMEM, VMEM, VMEM],
        out_specs=VMEM,
        compiler_params=params(),
        name="partial_product",
    )(where, half, order, top_rows, lower)


def add_kernel(slots, a_ref, b_ref, *outs):
    for m in range(slots):
        outs[m][...] = a_ref[m] + b_ref[m]


def add_slots(a, b):
    slots = a.shape[0]
    shape = jax.ShapeDtypeStruct(a.shape[1:], F32)
    return pl.pallas_call(
        functools.partial(add_kernel, slots),
        out_shape=(shape,) * slots,
        in_specs=[VMEM, VMEM],
        out_specs=(VMEM,) * slots,
        compiler_params=params(),
        name="add_slots",
    )(a, b)


def sum_kernel(*refs):
    total = refs[0][...]
    for r in refs[1:-1]:
        total = total + r[...]
    refs[-1][...] = total


def sum_slots(*parts):
    return pl.pallas_call(
        sum_kernel,
        out_shape=jax.ShapeDtypeStruct(parts[0].shape, F32),
        in_specs=[VMEM] * len(parts),
        out_specs=VMEM,
        compiler_params=params(),
        name="sum_slots",
    )(*parts)


def side_kernel(*refs):
    goal, nr, out = refs[-3:]
    total = refs[0][...]
    for r in refs[1:-3]:
        total = total + r[...]
    side = goal[...] - total
    n = nr.shape[1]
    for c in range(2):
        cols = slice(c * n, (c + 1) * n)
        out[:, cols] = block_dot(lhs(side[:, cols]), block_rhs(nr[c]))


def side_slot(parts, goal, new_right):
    return pl.pallas_call(
        side_kernel,
        out_shape=jax.ShapeDtypeStruct(goal.shape, F32),
        in_specs=[VMEM] * (len(parts) + 2),
        out_specs=VMEM,
        compiler_params=params(),
        name="side_slot",
    )(*parts, goal, new_right)


def rotate_kernel(slots, where, *refs):
    rs, (q_ref, out, buf) = refs[:slots], refs[slots:]
    blocks, n, _ = q_ref.shape
    for m in range(slots):
        depth = rs[m].shape[0]
        buf[pl.ds(pl.multiple_of((where[0] ^ m) * depth, 8), depth), :] = rs[m][...]
    for i in range(blocks):
        rows = slice(i * n, (i + 1) * n)
        out[rows, :] = wide_dot(lhs(q_ref[i]), wide_rhs(buf[rows, :]))


def rotate(where, parts, q):
    blocks, n, _ = q.shape
    shape = (blocks * n, parts[0].shape[1])
    return pl.pallas_call(
        functools.partial(rotate_kernel, len(parts)),
        out_shape=jax.ShapeDtypeStruct(shape, F32),
        in_specs=[SMEM] + [VMEM] * (len(parts) + 1),
        out_specs=VMEM,
        scratch_shapes=[pltpu.VMEM(shape, F32)],
        compiler_params=params(),
        name="rotate",
    )(where, *parts, q)


def own_kernel(row, u_ref, q_ref, p_ref, e_ref, nr_ref, nl_ref, diag_ref, s_ref, g_ref):
    blocks, n, _ = p_ref.shape
    p = [block_rhs(p_ref[k]) for k in range(blocks)]
    for i in range(blocks):
        q = lhs(q_ref[i])
        rows = slice(i * n, (i + 1) * n)
        s_ref[i] = block_dot(q, p[i])
        if i > 0:
            diag_ref[rows, : i * n] = jnp.zeros((n, i * n), F32)
        diag_ref[rows, i * n : (i + 1) * n] = jnp.zeros((n, n), F32)
        if i + 1 < blocks:
            qu = wide_dot(q, wide_rhs(u_ref[rows, (i + 1) * n :]))
        for k in range(i + 1, blocks):
            own = qu[:, (k - i - 1) * n : (k - i) * n]
            diag_ref[rows, k * n : (k + 1) * n] = block_dot(lhs(own), p[k])
    left = lhs(nl_ref[0])
    g_ref[0] = block_dot(left, block_rhs(nr_ref[0]))
    both = block_dot(left, block_rhs(e_ref[...]))
    g_ref[1] = block_dot(lhs(both), block_rhs(nr_ref[1]))
    g_ref[2] = block_dot(lhs(nl_ref[1]), block_rhs(nr_ref[1]))


def whole(a):
    return pl.BlockSpec(a.shape, lambda i, r: (0,) * a.ndim)


def prepare_own(row, corner, q, p, coupling, new_right, new_left):
    blocks, n, _ = q.shape
    half = blocks * n
    shapes = (
        jax.ShapeDtypeStruct((half, half), F32),
        jax.ShapeDtypeStruct(q.shape, F32),
        jax.ShapeDtypeStruct((3, n, n), F32),
    )
    return pl.pallas_call(
        own_kernel,
        out_shape=shapes,
        grid_spec=pltpu.PrefetchScalarGridSpec(
            num_scalar_prefetch=1,
            grid=(1,),
            in_specs=[
                pl.BlockSpec((half, half), lambda i, r: (0, r[0])),
                whole(q),
                whole(p),
                whole(coupling),
                whole(new_right),
                whole(new_left),
            ],
            out_specs=tuple(whole(a) for a in shapes),
        ),
        compiler_params=params(),
        name="prepare_own",
    )(row, corner, q, p, coupling, new_right, new_left)


def cross_kernel(row, u_ref, q_ref, p_ref, out_ref):
    blocks, n, _ = p_ref.shape
    q = lhs(q_ref[0])
    for k in range(0, blocks, 2):
        last = min(k + 2, blocks)
        u = u_ref[:, k * n : last * n]
        if last - k == 2:
            qu = wide_dot(q, wide_rhs(u))
        else:
            qu = block_dot(q, block_rhs(u))
        for j in range(k, last):
            own = lhs(qu[:, (j - k) * n : (j - k + 1) * n])
            out_ref[j] = lhs(block_dot(own, block_rhs(p_ref[j])))


def prepare_cross(row, corner, q, p_other):
    blocks, n, _ = q.shape
    half = blocks * n
    return pl.pallas_call(
        cross_kernel,
        out_shape=jax.ShapeDtypeStruct((blocks, half, 2 * n), BF16),
        grid_spec=pltpu.PrefetchScalarGridSpec(
            num_scalar_prefetch=1,
            grid=(blocks,),
            in_specs=[
                pl.BlockSpec((n, half), lambda i, r: (i, 1 - r[0])),
                pl.BlockSpec((1, n, n), lambda i, r: (i, 0, 0)),
                whole(p_other),
            ],
            out_specs=pl.BlockSpec((blocks, n, 2 * n), lambda i, r: (0, i, 0)),
        ),
        compiler_params=params(),
        name="prepare_cross",
    )(row, corner, q, p_other)


def chain_kernel(lower, *refs):
    if lower:
        c_ref, t_ref, s_ref, av_ref, bv_ref, g_ref, toff_ref, z_ref, w_ref, c_buf = refs
    else:
        c_ref, w_ref, t_ref, s_ref, av_ref, bv_ref, g_ref, z_ref, c_buf = refs
    blocks, n, _ = s_ref.shape
    left = slice(0, n)
    right = slice(n, 2 * n)

    def rows(i):
        return slice(i * n, (i + 1) * n)

    g0 = wide_rhs(cat([g_ref[0], g_ref[1]], 1))
    g1 = block_rhs(g_ref[2])
    av = av_ref[...]

    def inverse(i, c):
        own = jnp.transpose(jnp.broadcast_to(av[i : i + 1, :], (n, n)))
        return 1.0 / (own + jnp.broadcast_to(bv_ref[c : c + 1, :], (n, n)))

    if lower:
        c_buf[...] = c_ref[...]
    else:
        c_buf[...] = c_ref[...] - w_ref[...]
    for i in range(blocks - 1, -1, -1):
        z0 = c_buf[rows(i), left] * inverse(i, 0)
        z_ref[rows(i), left] = z0
        hj = wide_dot(lhs(z0), g0)
        h0 = hj[:, left]
        if i > 0:
            t = lhs(t_ref[rows(i - 1), rows(i)])
            c_buf[rows(i - 1), left] -= block_dot(t, block_rhs(h0))
        coupled = block_dot(lhs(s_ref[i]), block_rhs(hj[:, right]))
        z1 = (c_buf[rows(i), right] - coupled) * inverse(i, 1)
        z_ref[rows(i), right] = z1
        h1 = block_dot(lhs(z1), g1)
        if i > 0:
            c_buf[rows(i - 1), right] -= block_dot(t, block_rhs(h1))
        if lower or i > 1:
            h = wide_rhs(cat([h0, h1], 1))
        if i > 1:
            above = slice(0, (i - 1) * n)
            c_buf[above, :] -= wide_dot(lhs(t_ref[above, rows(i)]), h)
        if lower:
            update = wide_dot(toff_ref[i], h)
            if i == blocks - 1:
                w_ref[...] = update
            else:
                w_ref[...] += update


def chain(c, w, t, s, av, bv, g, toff):
    blocks, n, _ = s.shape
    lower = toff is not None
    shape = jax.ShapeDtypeStruct((blocks * n, 2 * n), F32)
    operands = [c] + ([] if lower else [w])
    operands += [t, s, av, bv, g] + ([toff] if lower else [])
    return pl.pallas_call(
        functools.partial(chain_kernel, lower),
        out_shape=(shape, shape) if lower else shape,
        in_specs=[VMEM] * len(operands),
        out_specs=(VMEM, VMEM) if lower else VMEM,
        scratch_shapes=[pltpu.VMEM(shape.shape, F32)],
        compiler_params=params(),
        name="chain_lower" if lower else "chain_upper",
    )(*operands)


def final_kernel(row, upper_ref, lower_ref, p_ref, nl_ref, out_ref):
    blocks, n, _ = p_ref.shape
    nl = [block_rhs(nl_ref[c]) for c in range(2)]

    def solve(z_ref):
        for i in range(blocks):
            rows = slice(i * n, (i + 1) * n)
            y = [
                block_dot(lhs(z_ref[rows, c * n : (c + 1) * n]), nl[c]) for c in range(2)
            ]
            out_ref[rows, :] = wide_dot(lhs(p_ref[i]), wide_rhs(cat(y, 1)))

    @pl.when(row[0] == 0)
    def _():
        solve(upper_ref)

    @pl.when(row[0] != 0)
    def _():
        solve(lower_ref)


def final(row, z_upper, z_lower, p, new_left):
    return pl.pallas_call(
        final_kernel,
        out_shape=jax.ShapeDtypeStruct(z_upper.shape, F32),
        in_specs=[SMEM] + [VMEM] * 4,
        out_specs=VMEM,
        compiler_params=params(),
        name="final",
    )(row, z_upper, z_lower, p, new_left)


def exchange(block, mask):
    route = [(i, i ^ mask) for i in range(lax.axis_size("col"))]
    return lax.ppermute(block, "col", route)


def swap_rows(block):
    return lax.ppermute(block, "row", [(0, 1), (1, 0)])


def body(
    top_rows, lower_new, block_order, corner, target, coupling,
    top_right, top_left, top_values, new_right, new_left, new_values,
):
    cols = lax.axis_size("col")
    half_rows = target.shape[0]
    slots = min(cols, 8)
    depth = half_rows // slots
    row = lax.axis_index("row")
    where = lax.axis_index("col") % slots
    row_s, other_s, where_s = row[None], (1 - row)[None], where[None]

    corner = pltpu.with_memory_space_constraint(corner, pltpu.HBM)
    theirs = partial_product(where_s, row_s, block_order, top_rows, lower_new, slots)
    theirs = swap_rows(theirs)
    ours = partial_product(where_s, other_s, block_order, top_rows, lower_new, slots)
    pieces = add_slots(ours, theirs)
    received = [exchange(pieces[m], m) for m in range(1, slots)]
    diag, s, g = prepare_own(
        row_s, corner, top_left, top_right, coupling, new_right, new_left
    )
    p_other = swap_rows(top_right)
    q_other = swap_rows(top_left)
    av_other = swap_rows(top_values)
    goal = swap_rows(lax.dynamic_slice_in_dim(target, where * depth, depth, 0))
    toff = prepare_cross(row_s, corner, top_left, p_other)
    diag_other = swap_rows(diag)
    s_other = swap_rows(s)

    total = sum_slots(pieces[0], *received)
    mask = slots
    last = []
    while mask < cols:
        moved = exchange(total, mask)
        if mask * 2 < cols:
            total = total + moved
        else:
            last = [moved]
        mask *= 2
    side = side_slot([total] + last, goal, new_right)
    parts = [side] + [exchange(side, m) for m in range(1, slots)]
    c_lower = rotate(where_s, parts, q_other)
    c_upper = swap_rows(c_lower)
    z_lower, w = chain(
        c_lower, None, diag_other, s_other, av_other, new_values, g, toff
    )
    z_lower = swap_rows(z_lower)
    z_upper = chain(c_upper, w, diag, s, top_values, new_values, g, None)
    return final(row_s, z_upper, z_lower, top_right, new_left)


def solution(mesh):
    placed = (
        P(None, ("col", "row")),
        P(("col", "row"), None),
        P(("col", "row"), None),
        P("row", None),
        P("row", None),
        P(),
        P("row", None, None),
        P("row", None, None),
        P("row", None),
        P(),
        P(),
        P(),
    )
    return jax.shard_map(
        body, mesh=mesh, in_specs=placed, out_specs=P("row", None), check_vma=False
    )
```

profile of v0, /device:TPU:1, one launch (start us, length us, event | category | flops | bytes accessed | tf_op | source)
XLA Modules:
  0.0 84.7 jit_solution(11371449537166229515)
XLA Ops:
  0.0 1.1 %copy-done.2 = f32[7,128,128]{2,1,0:T(8,128)S(1)} copy-done((f32[7,128,128]{2,1,0:T(8,128)S(1)}, f32[7,128,128]{2,1,0:T(8,128)}, u32[]{:S(2)}) %copy-start.2) | copy-done | bytes 458776
  1.1 0.9 %copy-done.7 = f32[2,128,128]{2,1,0:T(8,128)S(1)} copy-done((f32[2,128,128]{2,1,0:T(8,128)S(1)}, f32[2,128,128]{2,1,0:T(8,128)}, u32[]{:S(2)}) %copy-start.7) | copy-done | bytes 131096
  2.0 0.9 %copy-done.9 = f32[2,128,128]{2,1,0:T(8,128)S(1)} copy-done((f32[2,128,128]{2,1,0:T(8,128)S(1)}, f32[2,128,128]{2,1,0:T(8,128)}, u32[]{:S(2)}) %copy-start.9) | copy-done | bytes 131096
  2.9 0.8 copy-done.13
  3.8 5.6 %prepare_own.1 = (f32[896,896]{1,0:T(8,128)}, f32[7,128,128]{2,1,0:T(8,128)S(1)}, f32[3,128,128]{2,1,0:T(8,128)S(1)}) custom-call(s32[1]{0:T(128)} %bitcast.half.row, f32[896,1792]{1,0:T(8,128)} %u_ref.3, f32[7,128,128]{2,1,0:T(8,128)} %q_ref.3, f32[7,128,128]{2,1,0:T(8,128)S(1)} %copy-done.2, f32[128,128]{1,0:T(8,128)S(1)} %copy-done.13, ...), custom_call_target="tpu_custom_call" | custom-call | tf_op jit(solution)/shard_map/prepare_own/pallas_call | solution.py:205
  9.4 0.7 copy-done.5
  10.1 0.8 copy-done.11
  10.9 0.0 collective-permute-start.19
  10.9 2.1 %partial_product.3 = f32[8,112,256]{2,1,0:T(8,128)} custom-call(s32[1]{0:T(128)} %bitcast.1.where, s32[1]{0:T(128)} %bitcast.half.row, s32[1,2]{1,0:T(1,128)S(1)} %copy-done.16, f32[1792,256]{1,0:T(8,128)S(1)} %copy-done.1, f32[256,256]{1,0:T(8,128)S(1)} %copy-done.4), custom_call_target="tpu_custom_call" | custom-call | tf_op jit(solution)/shard_map/partial_product/pallas_call | solution.py:77
  13.0 0.5 collective-permute-start
  13.5 1.2 %partial_product.2.a_ref = f32[8,112,256]{2,1,0:T(8,128)S(1)} custom-call(s32[1]{0:T(128)} %bitcast.1.where, s32[1]{0:T(128)} %bitcast.2.half, s32[1,2]{1,0:T(1,128)S(1)} %copy-done.16, f32[1792,256]{1,0:T(8,128)S(1)} %copy-done.1, f32[256,256]{1,0:T(8,128)S(1)} %copy-done.4), custom_call_target="tpu_custom_call" | custom-call | tf_op jit(solution)/shard_map/partial_product/pallas_call | solution.py:77
  14.6 3.6 %collective-permute-done.b_ref = f32[8,112,256]{2,1,0:T(8,128)} collective-permute-done((f32[8,112,256]{2,1,0:T(8,128)}, f32[8,112,256]{2,1,0:T(8,128)}, u32[]{:S(2)}, u32[]{:S(2)}) %collective-permute-start) | collective-permute-done | bytes 917536 | tf_op jit(solution)/shard_map/ppermute | solution.py:368
  18.3 1.3 %add_slots.1 = (f32[112,256]{1,0:T(8,128)S(1)}, f32[112,256]{1,0:T(8,128)S(1)}, f32[112,256]{1,0:T(8,128)S(1)}, f32[112,256]{1,0:T(8,128)S(1)}, f32[112,256]{1,0...) custom-call(f32[8,112,256]{2,1,0:T(8,128)S(1)} %partial_product.2.a_ref, ...), custom_call_target="tpu_custom_call" | custom-call | tf_op jit(solution)/shard_map/add_slots/pallas_call | solution.py:95
  19.6 2.4 %collective-permute-start.1 = (f32[112,256]{1,0:T(8,128)S(1)}, f32[112,256]{1,0:T(8,128)S(1)}, u32[]{:S(2)}, u32[]{:S(2)}) collective-permute-start(f32[112,256]{1,0:T(8,128)S(1)} %get-tuple-element.19), channel_id=1, source_target_pairs={{0,2},{2,0},{4,6},{6,4},{8,10},{10,8},{12,14},{14,12},{16,18},{18,... | collective-permute-start | bytes 344072 | tf_op jit(solution)/shard_map/ppermute | solution.py:364
  22.0 1.2 %collective-permute-start.2 = (f32[112,256]{1,0:T(8,128)S(1)}, f32[112,256]{1,0:T(8,128)S(1)}, u32[]{:S(2)}, u32[]{:S(2)}) collective-permute-start(f32[112,256]{1,0:T(8,128)S(1)} %get-tuple-element.20), channel_id=1, source_target_pairs={{0,4},{2,6},{4,0},{6,2},{8,12},{10,14},{12,8},{14,10},{16,20},{18,... | collective-permute-start | bytes 344072 | tf_op jit(solution)/shard_map/ppermute | solution.py:364
  23.2 0.0 collective-permute-start.3
  23.2 1.5 %collective-permute-start.4 = (f32[112,256]{1,0:T(8,128)S(1)}, f32[112,256]{1,0:T(8,128)S(1)}, u32[]{:S(2)}, u32[]{:S(2)}) collective-permute-start(f32[112,256]{1,0:T(8,128)S(1)} %get-tuple-element.22), channel_id=1, source_target_pairs={{0,8},{2,10},{4,12},{6,14},{8,0},{10,2},{12,4},{14,6},{16,24},{18,... | collective-permute-start | bytes 344072 | tf_op jit(solution)/shard_map/ppermute | solution.py:364
  24.7 0.4 collective-permute-done.1.refs_1_
  25.1 2.2 %collective-permute-start.5 = (f32[112,256]{1,0:T(8,128)S(1)}, f32[112,256]{1,0:T(8,128)S(1)}, u32[]{:S(2)}, u32[]{:S(2)}) collective-permute-start(f32[112,256]{1,0:T(8,128)S(1)} %get-tuple-element.23), channel_id=1, source_target_pairs={{0,10},{2,8},{4,14},{6,12},{8,2},{10,0},{12,6},{14,4},{16,26},{18,... | collective-permute-start | bytes 344072 | tf_op jit(solution)/shard_map/ppermute | solution.py:364
  27.3 2.7 %collective-permute-start.17 = (f32[7,128,128]{2,1,0:T(8,128)}, f32[7,128,128]{2,1,0:T(8,128)S(1)}, u32[]{:S(2)}, u32[]{:S(2)}) collective-permute-start(f32[7,128,128]{2,1,0:T(8,128)} %q_ref.3), channel_id=1, source_target_pairs={{0,1},{1,0},{2,3},{3,2},{4,5},{5,4},{6,7},{7,6},{8,9},{9,8},{10,11... | collective-permute-start | bytes 1376264 | tf_op jit(solution)/shard_map/ppermute | solution.py:368
  30.0 0.1 collective-permute-start.22
  30.1 0.0 collective-permute-done.4.refs_4_
  30.1 2.3 %collective-permute-start.6 = (f32[112,256]{1,0:T(8,128)S(1)}, f32[112,256]{1,0:T(8,128)S(1)}, u32[]{:S(2)}, u32[]{:S(2)}) collective-permute-start(f32[112,256]{1,0:T(8,128)S(1)} %get-tuple-element.24), channel_id=1, source_target_pairs={{0,12},{2,14},{4,8},{6,10},{8,4},{10,6},{12,0},{14,2},{16,28},{18,... | collective-permute-start | bytes 344072 | tf_op jit(solution)/shard_map/ppermute | solution.py:364
  32.3 0.8 collective-permute-start.7
  33.1 2.1 %collective-permute-done.6.refs_6_ = f32[112,256]{1,0:T(8,128)S(1)} collective-permute-done((f32[112,256]{1,0:T(8,128)S(1)}, f32[112,256]{1,0:T(8,128)S(1)}, u32[]{:S(2)}, u32[]{:S(2)}) %collective-permute-start.6) | collective-permute-done | bytes 114720 | tf_op jit(solution)/shard_map/ppermute | solution.py:364
  35.2 1.5 %collective-permute-start.9 = (f32[112,256]{1,0:T(8,128)S(1)}, f32[112,256]{1,0:T(8,128)S(1)}, u32[]{:S(2)}, u32[]{:S(2)}) collective-permute-start(f32[112,256]{1,0:T(8,128)S(1)} %constant_dynamic-slice_fusion), channel_id=1, source_target_pairs={{0,1},{1,0},{2,3},{3,2},{4,5},{5,4},{6,7},{7,6},{8,9},{9,8},{10,11... | collective-permute-start | bytes 344072 | tf_op jit(solution)/shard_map/ppermute | solution.py:368
  36.8 1.4 %collective-permute-done.7.refs_7_ = f32[112,256]{1,0:T(8,128)S(1)} collective-permute-done((f32[112,256]{1,0:T(8,128)S(1)}, f32[112,256]{1,0:T(8,128)S(1)}, u32[]{:S(2)}, u32[]{:S(2)}) %collective-permute-start.7) | collective-permute-done | bytes 114720 | tf_op jit(solution)/shard_map/ppermute | solution.py:364
  38.2 2.4 %collective-permute-start.8 = (f32[112,256]{1,0:T(8,128)S(1)}, f32[112,256]{1,0:T(8,128)S(1)}, u32[]{:S(2)}, u32[]{:S(2)}) collective-permute-start(f32[112,256]{1,0:T(8,128)S(1)} %sum_slots.1.refs_0_), channel_id=1, source_target_pairs={{0,16},{2,18},{4,20},{6,22},{8,24},{10,26},{12,28},{14,30},{16,0},... | collective-permute-start | bytes 344072 | tf_op jit(solution)/shard_map/ppermute | solution.py:364
  40.5 1.8 %collective-permute-start.20 = (f32[7,128,128]{2,1,0:T(8,128)}, f32[7,128,128]{2,1,0:T(8,128)S(1)}, u32[]{:S(2)}, u32[]{:S(2)}) collective-permute-start(f32[7,128,128]{2,1,0:T(8,128)} %copy-done.11), channel_id=1, source_target_pairs={{0,1},{1,0},{2,3},{3,2},{4,5},{5,4},{6,7},{7,6},{8,9},{9,8},{10,11... | collective-permute-start | bytes 1376264 | tf_op jit(solution)/shard_map/ppermute | solution.py:368
  42.4 2.0 %collective-permute-done.8.refs_1_ = f32[112,256]{1,0:T(8,128)S(1)} collective-permute-done((f32[112,256]{1,0:T(8,128)S(1)}, f32[112,256]{1,0:T(8,128)S(1)}, u32[]{:S(2)}, u32[]{:S(2)}) %collective-permute-start.8) | collective-permute-done | bytes 114720 | tf_op jit(solution)/shard_map/ppermute | solution.py:364
  44.4 0.2 side_slot.1.refs_0_
  44.6 0.0 copy-start.15
  44.6 0.1 collective-permute-start.10
  44.7 3.1 %collective-permute-start.11 = (f32[112,256]{1,0:T(8,128)S(1)}, f32[112,256]{1,0:T(8,128)S(1)}, u32[]{:S(2)}, u32[]{:S(2)}) collective-permute-start(f32[112,256]{1,0:T(8,128)S(1)} %side_slot.1.refs_0_), channel_id=1, source_target_pairs={{0,4},{2,6},{4,0},{6,2},{8,12},{10,14},{12,8},{14,10},{16,20},{18,... | collective-permute-start | bytes 344072 | tf_op jit(solution)/shard_map/ppermute | solution.py:364
  47.9 1.2 %collective-permute-start.12 = (f32[112,256]{1,0:T(8,128)S(1)}, f32[112,256]{1,0:T(8,128)S(1)}, u32[]{:S(2)}, u32[]{:S(2)}) collective-permute-start(f32[112,256]{1,0:T(8,128)S(1)} %side_slot.1.refs_0_), channel_id=1, source_target_pairs={{0,6},{2,4},{4,2},{6,0},{8,14},{10,12},{12,10},{14,8},{16,22},{18,... | collective-permute-start | bytes 344072 | tf_op jit(solution)/shard_map/ppermute | solution.py:364
  49.0 1.0 %collective-permute-start.13 = (f32[112,256]{1,0:T(8,128)S(1)}, f32[112,256]{1,0:T(8,128)S(1)}, u32[]{:S(2)}, u32[]{:S(2)}) collective-permute-start(f32[112,256]{1,0:T(8,128)S(1)} %side_slot.1.refs_0_), channel_id=1, source_target_pairs={{0,8},{2,10},{4,12},{6,14},{8,0},{10,2},{12,4},{14,6},{16,24},{18,... | collective-permute-start | bytes 344072 | tf_op jit(solution)/shard_map/ppermute | solution.py:364
  50.0 2.8 %collective-permute-start.14 = (f32[112,256]{1,0:T(8,128)S(1)}, f32[112,256]{1,0:T(8,128)S(1)}, u32[]{:S(2)}, u32[]{:S(2)}) collective-permute-start(f32[112,256]{1,0:T(8,128)S(1)} %side_slot.1.refs_0_), channel_id=1, source_target_pairs={{0,10},{2,8},{4,14},{6,12},{8,2},{10,0},{12,6},{14,4},{16,26},{18,... | collective-permute-start | bytes 344072 | tf_op jit(solution)/shard_map/ppermute | solution.py:364
  52.9 0.5 collective-permute-done.12.refs_3_
  53.4 0.9 %collective-permute-start.15 = (f32[112,256]{1,0:T(8,128)S(1)}, f32[112,256]{1,0:T(8,128)S(1)}, u32[]{:S(2)}, u32[]{:S(2)}) collective-permute-start(f32[112,256]{1,0:T(8,128)S(1)} %side_slot.1.refs_0_), channel_id=1, source_target_pairs={{0,12},{2,14},{4,8},{6,10},{8,4},{10,6},{12,0},{14,2},{16,28},{18,... | collective-permute-start | bytes 344072 | tf_op jit(solution)/shard_map/ppermute | solution.py:364
  54.3 2.1 %collective-permute-start.16 = (f32[112,256]{1,0:T(8,128)S(1)}, f32[112,256]{1,0:T(8,128)S(1)}, u32[]{:S(2)}, u32[]{:S(2)}) collective-permute-start(f32[112,256]{1,0:T(8,128)S(1)} %side_slot.1.refs_0_), channel_id=1, source_target_pairs={{0,14},{2,12},{4,10},{6,8},{8,6},{10,4},{12,2},{14,0},{16,30},{18,... | collective-permute-start | bytes 344072 | tf_op jit(solution)/shard_map/ppermute | solution.py:364
  56.4 5.3 %collective-permute-start.21 = (f32[7,128]{1,0:T(8,128)S(1)}, f32[7,128]{1,0:T(8,128)S(1)}, u32[]{:S(2)}, u32[]{:S(2)}) collective-permute-start(f32[7,128]{1,0:T(8,128)S(1)} %copy-done.14), channel_id=1, source_target_pairs={{0,1},{1,0},{2,3},{3,2},{4,5},{5,4},{6,7},{7,6},{8,9},{9,8},{10,11... | collective-permute-start | bytes 10760 | tf_op jit(solution)/shard_map/ppermute | solution.py:368
  61.8 6.4 %prepare_cross.1.refs_6_ = bf16[7,896,256]{2,1,0:T(8,128)(2,1)S(1)} custom-call(s32[1]{0:T(128)} %bitcast.half.row, f32[896,1792]{1,0:T(8,128)} %u_ref.3, f32[7,128,128]{2,1,0:T(8,128)} %q_ref.3, f32[7,128,128]{2,1,0:T(8,128)S(1)} %collective-permute-done.22.p_ref), custom_call_target="tpu_custom_call" | custom-call | tf_op jit(solution)/shard_map/prepare_cross/pallas_call | solution.py:244
  68.1 0.5 rotate.1.refs_0_
  68.6 0.1 collective-permute-start.18
  68.8 8.1 %chain_lower.1 = (f32[896,256]{1,0:T(8,128)S(1)}, f32[896,256]{1,0:T(8,128)S(1)}) custom-call(f32[896,256]{1,0:T(8,128)S(1)} %rotate.1.refs_0_, f32[896,896]{1,0:T(8,128)} %collective-permute-done.19.refs_1_, f32[7,128,128]{2,1,0:T(8,128)S(1)} %collective-permute-done.20.refs_2_, f32[7,128]{1,0:T(8,128)S(1)} %collective-permute-done.21.refs_3_, ...), custom_call_target="tpu_custom_call" | custom-call | tf_op jit(solution)/shard_map/chain_lower/pallas_call | solution.py:319
  76.9 0.5 collective-permute-start.23
  77.4 5.5 %chain_upper.1.upper_ref = f32[896,256]{1,0:T(8,128)S(1)} custom-call(f32[896,256]{1,0:T(8,128)S(1)} %collective-permute-done.18.refs_0_, f32[896,256]{1,0:T(8,128)S(1)} %get-tuple-element.29.refs_1_, f32[896,896]{1,0:T(8,128)} %get-tuple-element.26.refs_2_, f32[7,128,128]{2,1,0:T(8,128)S(1)} %copy-done.12, f32[7,128]{1,0:T(8,128)S(1)} %copy-done.14, ...), custom_call_target="tpu_custom_call" | custom-call | tf_op jit(solution)/shard_map/chain_upper/pallas_call | solution.py:319
  82.9 1.8 %final.1 = f32[896,256]{1,0:T(8,128)} custom-call(s32[1]{0:T(128)} %bitcast.half.row, f32[896,256]{1,0:T(8,128)S(1)} %chain_upper.1.upper_ref, f32[896,256]{1,0:T(8,128)S(1)} %collective-permute-done.23.lower_ref, f32[7,128,128]{2,1,0:T(8,128)S(1)} %copy-done.3, f32[2,128,128]{2,1,0:T(8,128)S(1)} %copy-done.8), custom_call_target="tpu_custom_call" | custom-call | tf_op jit(solution)/shard_map/final/pallas_call | solution.py:352
  (46 shorter events, 0.1 us)
Async XLA Ops:
  0.0 33.1 %copy-start = (f32[896,256]{1,0:T(8,128)S(1)}, f32[896,256]{1,0:T(8,128)}, u32[]{:S(2)}) copy-start(f32[896,256]{1,0:T(8,128)} %param.16) | copy-start | bytes 2752516
  0.0 1.1 %copy-start.2 = (f32[7,128,128]{2,1,0:T(8,128)S(1)}, f32[7,128,128]{2,1,0:T(8,128)}, u32[]{:S(2)}) copy-start(f32[7,128,128]{2,1,0:T(8,128)} %p_ref.3) | copy-start | bytes 1376260
  1.1 0.9 %copy-start.7 = (f32[2,128,128]{2,1,0:T(8,128)S(1)}, f32[2,128,128]{2,1,0:T(8,128)}, u32[]{:S(2)}) copy-start(f32[2,128,128]{2,1,0:T(8,128)} %nl_ref.3) | copy-start | bytes 393220
  2.0 0.9 %copy-start.9 = (f32[2,128,128]{2,1,0:T(8,128)S(1)}, f32[2,128,128]{2,1,0:T(8,128)}, u32[]{:S(2)}) copy-start(f32[2,128,128]{2,1,0:T(8,128)} %nr_ref.1) | copy-start | bytes 393220
  2.9 0.8 copy-start.13
  3.8 7.1 %copy-start.1 = (f32[1792,256]{1,0:T(8,128)S(1)}, f32[1792,256]{1,0:T(8,128)}, u32[]{:S(2)}) copy-start(f32[1792,256]{1,0:T(8,128)} %a_ref.3) | copy-start | bytes 5505028
  3.8 7.1 %copy-start.4 = (f32[256,256]{1,0:T(8,128)S(1)}, f32[256,256]{1,0:T(8,128)}, u32[]{:S(2)}) copy-start(f32[256,256]{1,0:T(8,128)} %b_ref.3) | copy-start | bytes 786436
  3.8 7.1 %copy-start.16 = (s32[1,2]{1,0:T(1,128)S(1)}, s32[1,2]{1,0:T(1,128)}, u32[]{:S(2)}) copy-start(s32[1,2]{1,0:T(1,128)} %order.3) | copy-start | bytes 28
  9.4 0.7 copy-start.5
  10.1 0.8 copy-start.11
  10.9 57.9 %collective-permute-start.19 = (f32[896,896]{1,0:T(8,128)}, f32[896,896]{1,0:T(8,128)}, u32[]{:S(2)}, u32[]{:S(2)}) collective-permute-start(f32[896,896]{1,0:T(8,128)} %get-tuple-element.26.refs_2_), channel_id=1, source_target_pairs={{0,1},{1,0},{2,3},{3,2},{4,5},{5,4},{6,7},{7,6},{8,9},{9,8},{10,11... | collective-permute-start | bytes 9633800 | tf_op jit(solution)/shard_map/ppermute | solution.py:368
  10.9 19.1 %copy-start.3 = (f32[7,128,128]{2,1,0:T(8,128)S(1)}, f32[7,128,128]{2,1,0:T(8,128)}, u32[]{:S(2)}) copy-start(f32[7,128,128]{2,1,0:T(8,128)} %p_ref.3) | copy-start | bytes 1376260
  13.0 5.3 %collective-permute-start = (f32[8,112,256]{2,1,0:T(8,128)}, f32[8,112,256]{2,1,0:T(8,128)}, u32[]{:S(2)}, u32[]{:S(2)}) collective-permute-start(f32[8,112,256]{2,1,0:T(8,128)} %partial_product.3), channel_id=1, source_target_pairs={{0,1},{1,0},{2,3},{3,2},{4,5},{5,4},{6,7},{7,6},{8,9},{9,8},{10,11... | collective-permute-start | bytes 2752520 | tf_op jit(solution)/shard_map/ppermute | solution.py:368
  13.5 43.0 %copy-start.14 = (f32[7,128]{1,0:T(8,128)S(1)}, f32[7,128]{1,0:T(8,128)}, u32[]{:S(2)}) copy-start(f32[7,128]{1,0:T(8,128)} %refs_4_.3) | copy-start | bytes 10756
  14.6 29.8 %copy-start.10 = (f32[2,128,128]{2,1,0:T(8,128)S(1)}, f32[2,128,128]{2,1,0:T(8,128)}, u32[]{:S(2)}) copy-start(f32[2,128,128]{2,1,0:T(8,128)} %nr_ref.1) | copy-start | bytes 393220
  19.6 5.6 %collective-permute-start.1 = (f32[112,256]{1,0:T(8,128)S(1)}, f32[112,256]{1,0:T(8,128)S(1)}, u32[]{:S(2)}, u32[]{:S(2)}) collective-permute-start(f32[112,256]{1,0:T(8,128)S(1)} %get-tuple-element.19), channel_id=1, source_target_pairs={{0,2},{2,0},{4,6},{6,4},{8,10},{10,8},{12,14},{14,12},{16,18},{18,... | collective-permute-start | bytes 344072 | tf_op jit(solution)/shard_map/ppermute | solution.py:364
  22.0 5.3 %collective-permute-start.2 = (f32[112,256]{1,0:T(8,128)S(1)}, f32[112,256]{1,0:T(8,128)S(1)}, u32[]{:S(2)}, u32[]{:S(2)}) collective-permute-start(f32[112,256]{1,0:T(8,128)S(1)} %get-tuple-element.20), channel_id=1, source_target_pairs={{0,4},{2,6},{4,0},{6,2},{8,12},{10,14},{12,8},{14,10},{16,20},{18,... | collective-permute-start | bytes 344072 | tf_op jit(solution)/shard_map/ppermute | solution.py:364
  23.2 6.8 %collective-permute-start.3 = (f32[112,256]{1,0:T(8,128)S(1)}, f32[112,256]{1,0:T(8,128)S(1)}, u32[]{:S(2)}, u32[]{:S(2)}) collective-permute-start(f32[112,256]{1,0:T(8,128)S(1)} %get-tuple-element.21), channel_id=1, source_target_pairs={{0,6},{2,4},{4,2},{6,0},{8,14},{10,12},{12,10},{14,8},{16,22},{18,... | collective-permute-start | bytes 344072 | tf_op jit(solution)/shard_map/ppermute | solution.py:364
  23.2 6.8 %collective-permute-start.4 = (f32[112,256]{1,0:T(8,128)S(1)}, f32[112,256]{1,0:T(8,128)S(1)}, u32[]{:S(2)}, u32[]{:S(2)}) collective-permute-start(f32[112,256]{1,0:T(8,128)S(1)} %get-tuple-element.22), channel_id=1, source_target_pairs={{0,8},{2,10},{4,12},{6,14},{8,0},{10,2},{12,4},{14,6},{16,24},{18,... | collective-permute-start | bytes 344072 | tf_op jit(solution)/shard_map/ppermute | solution.py:364
  25.1 7.2 %collective-permute-start.5 = (f32[112,256]{1,0:T(8,128)S(1)}, f32[112,256]{1,0:T(8,128)S(1)}, u32[]{:S(2)}, u32[]{:S(2)}) collective-permute-start(f32[112,256]{1,0:T(8,128)S(1)} %get-tuple-element.23), channel_id=1, source_target_pairs={{0,10},{2,8},{4,14},{6,12},{8,2},{10,0},{12,6},{14,4},{16,26},{18,... | collective-permute-start | bytes 344072 | tf_op jit(solution)/shard_map/ppermute | solution.py:364
  27.3 17.4 %collective-permute-start.17 = (f32[7,128,128]{2,1,0:T(8,128)}, f32[7,128,128]{2,1,0:T(8,128)S(1)}, u32[]{:S(2)}, u32[]{:S(2)}) collective-permute-start(f32[7,128,128]{2,1,0:T(8,128)} %q_ref.3), channel_id=1, source_target_pairs={{0,1},{1,0},{2,3},{3,2},{4,5},{5,4},{6,7},{7,6},{8,9},{9,8},{10,11... | collective-permute-start | bytes 1376264 | tf_op jit(solution)/shard_map/ppermute | solution.py:368
  30.0 17.9 %collective-permute-start.22 = (f32[7,128,128]{2,1,0:T(8,128)S(1)}, f32[7,128,128]{2,1,0:T(8,128)S(1)}, u32[]{:S(2)}, u32[]{:S(2)}) collective-permute-start(f32[7,128,128]{2,1,0:T(8,128)S(1)} %copy-done.3), channel_id=1, source_target_pairs={{0,1},{1,0},{2,3},{3,2},{4,5},{5,4},{6,7},{7,6},{8,9},{9,8},{10,11... | collective-permute-start | bytes 1376264 | tf_op jit(solution)/shard_map/ppermute | solution.py:368
  30.1 5.2 %collective-permute-start.6 = (f32[112,256]{1,0:T(8,128)S(1)}, f32[112,256]{1,0:T(8,128)S(1)}, u32[]{:S(2)}, u32[]{:S(2)}) collective-permute-start(f32[112,256]{1,0:T(8,128)S(1)} %get-tuple-element.24), channel_id=1, source_target_pairs={{0,12},{2,14},{4,8},{6,10},{8,4},{10,6},{12,0},{14,2},{16,28},{18,... | collective-permute-start | bytes 344072 | tf_op jit(solution)/shard_map/ppermute | solution.py:364
  32.3 5.8 %collective-permute-start.7 = (f32[112,256]{1,0:T(8,128)S(1)}, f32[112,256]{1,0:T(8,128)S(1)}, u32[]{:S(2)}, u32[]{:S(2)}) collective-permute-start(f32[112,256]{1,0:T(8,128)S(1)} %get-tuple-element.25), channel_id=1, source_target_pairs={{0,14},{2,12},{4,10},{6,8},{8,6},{10,4},{12,2},{14,0},{16,30},{18,... | collective-permute-start | bytes 344072 | tf_op jit(solution)/shard_map/ppermute | solution.py:364
  35.2 5.3 %collective-permute-start.9 = (f32[112,256]{1,0:T(8,128)S(1)}, f32[112,256]{1,0:T(8,128)S(1)}, u32[]{:S(2)}, u32[]{:S(2)}) collective-permute-start(f32[112,256]{1,0:T(8,128)S(1)} %constant_dynamic-slice_fusion), channel_id=1, source_target_pairs={{0,1},{1,0},{2,3},{3,2},{4,5},{5,4},{6,7},{7,6},{8,9},{9,8},{10,11... | collective-permute-start | bytes 344072 | tf_op jit(solution)/shard_map/ppermute | solution.py:368
  38.2 6.2 %collective-permute-start.8 = (f32[112,256]{1,0:T(8,128)S(1)}, f32[112,256]{1,0:T(8,128)S(1)}, u32[]{:S(2)}, u32[]{:S(2)}) collective-permute-start(f32[112,256]{1,0:T(8,128)S(1)} %sum_slots.1.refs_0_), channel_id=1, source_target_pairs={{0,16},{2,18},{4,20},{6,22},{8,24},{10,26},{12,28},{14,30},{16,0},... | collective-permute-start | bytes 344072 | tf_op jit(solution)/shard_map/ppermute | solution.py:364
  40.5 28.2 %collective-permute-start.20 = (f32[7,128,128]{2,1,0:T(8,128)}, f32[7,128,128]{2,1,0:T(8,128)S(1)}, u32[]{:S(2)}, u32[]{:S(2)}) collective-permute-start(f32[7,128,128]{2,1,0:T(8,128)} %copy-done.11), channel_id=1, source_target_pairs={{0,1},{1,0},{2,3},{3,2},{4,5},{5,4},{6,7},{7,6},{8,9},{9,8},{10,11... | collective-permute-start | bytes 1376264 | tf_op jit(solution)/shard_map/ppermute | solution.py:368
  44.6 24.1 %copy-start.6 = (f32[3,128,128]{2,1,0:T(8,128)S(1)}, f32[3,128,128]{2,1,0:T(8,128)}, u32[]{:S(2)}) copy-start(f32[3,128,128]{2,1,0:T(8,128)} %copy-done.5) | copy-start | bytes 589828
  44.6 24.1 %copy-start.15 = (f32[2,128]{1,0:T(2,128)S(1)}, f32[2,128]{1,0:T(2,128)}, u32[]{:S(2)}) copy-start(f32[2,128]{1,0:T(2,128)} %refs_5_.1) | copy-start | bytes 3076
  44.6 4.4 %collective-permute-start.10 = (f32[112,256]{1,0:T(8,128)S(1)}, f32[112,256]{1,0:T(8,128)S(1)}, u32[]{:S(2)}, u32[]{:S(2)}) collective-permute-start(f32[112,256]{1,0:T(8,128)S(1)} %side_slot.1.refs_0_), channel_id=1, source_target_pairs={{0,2},{2,0},{4,6},{6,4},{8,10},{10,8},{12,14},{14,12},{16,18},{18,... | collective-permute-start | bytes 344072 | tf_op jit(solution)/shard_map/ppermute | solution.py:364
  44.7 5.3 %collective-permute-start.11 = (f32[112,256]{1,0:T(8,128)S(1)}, f32[112,256]{1,0:T(8,128)S(1)}, u32[]{:S(2)}, u32[]{:S(2)}) collective-permute-start(f32[112,256]{1,0:T(8,128)S(1)} %side_slot.1.refs_0_), channel_id=1, source_target_pairs={{0,4},{2,6},{4,0},{6,2},{8,12},{10,14},{12,8},{14,10},{16,20},{18,... | collective-permute-start | bytes 344072 | tf_op jit(solution)/shard_map/ppermute | solution.py:364
  47.9 5.5 %collective-permute-start.12 = (f32[112,256]{1,0:T(8,128)S(1)}, f32[112,256]{1,0:T(8,128)S(1)}, u32[]{:S(2)}, u32[]{:S(2)}) collective-permute-start(f32[112,256]{1,0:T(8,128)S(1)} %side_slot.1.refs_0_), channel_id=1, source_target_pairs={{0,6},{2,4},{4,2},{6,0},{8,14},{10,12},{12,10},{14,8},{16,22},{18,... | collective-permute-start | bytes 344072 | tf_op jit(solution)/shard_map/ppermute | solution.py:364
  49.0 5.3 %collective-permute-start.13 = (f32[112,256]{1,0:T(8,128)S(1)}, f32[112,256]{1,0:T(8,128)S(1)}, u32[]{:S(2)}, u32[]{:S(2)}) collective-permute-start(f32[112,256]{1,0:T(8,128)S(1)} %side_slot.1.refs_0_), channel_id=1, source_target_pairs={{0,8},{2,10},{4,12},{6,14},{8,0},{10,2},{12,4},{14,6},{16,24},{18,... | collective-permute-start | bytes 344072 | tf_op jit(solution)/shard_map/ppermute | solution.py:364
  50.0 6.4 %collective-permute-start.14 = (f32[112,256]{1,0:T(8,128)S(1)}, f32[112,256]{1,0:T(8,128)S(1)}, u32[]{:S(2)}, u32[]{:S(2)}) collective-permute-start(f32[112,256]{1,0:T(8,128)S(1)} %side_slot.1.refs_0_), channel_id=1, source_target_pairs={{0,10},{2,8},{4,14},{6,12},{8,2},{10,0},{12,6},{14,4},{16,26},{18,... | collective-permute-start | bytes 344072 | tf_op jit(solution)/shard_map/ppermute | solution.py:364
  53.4 14.7 %collective-permute-start.15 = (f32[112,256]{1,0:T(8,128)S(1)}, f32[112,256]{1,0:T(8,128)S(1)}, u32[]{:S(2)}, u32[]{:S(2)}) collective-permute-start(f32[112,256]{1,0:T(8,128)S(1)} %side_slot.1.refs_0_), channel_id=1, source_target_pairs={{0,12},{2,14},{4,8},{6,10},{8,4},{10,6},{12,0},{14,2},{16,28},{18,... | collective-permute-start | bytes 344072 | tf_op jit(solution)/shard_map/ppermute | solution.py:364
  54.3 13.8 %collective-permute-start.16 = (f32[112,256]{1,0:T(8,128)S(1)}, f32[112,256]{1,0:T(8,128)S(1)}, u32[]{:S(2)}, u32[]{:S(2)}) collective-permute-start(f32[112,256]{1,0:T(8,128)S(1)} %side_slot.1.refs_0_), channel_id=1, source_target_pairs={{0,14},{2,12},{4,10},{6,8},{8,6},{10,4},{12,2},{14,0},{16,30},{18,... | collective-permute-start | bytes 344072 | tf_op jit(solution)/shard_map/ppermute | solution.py:364
  56.4 12.3 %collective-permute-start.21 = (f32[7,128]{1,0:T(8,128)S(1)}, f32[7,128]{1,0:T(8,128)S(1)}, u32[]{:S(2)}, u32[]{:S(2)}) collective-permute-start(f32[7,128]{1,0:T(8,128)S(1)} %copy-done.14), channel_id=1, source_target_pairs={{0,1},{1,0},{2,3},{3,2},{4,5},{5,4},{6,7},{7,6},{8,9},{9,8},{10,11... | collective-permute-start | bytes 10760 | tf_op jit(solution)/shard_map/ppermute | solution.py:368
  68.6 8.8 %collective-permute-start.18 = (f32[896,256]{1,0:T(8,128)S(1)}, f32[896,256]{1,0:T(8,128)S(1)}, u32[]{:S(2)}, u32[]{:S(2)}) collective-permute-start(f32[896,256]{1,0:T(8,128)S(1)} %rotate.1.refs_0_), channel_id=1, source_target_pairs={{0,1},{1,0},{2,3},{3,2},{4,5},{5,4},{6,7},{7,6},{8,9},{9,8},{10,11... | collective-permute-start | bytes 2752520 | tf_op jit(solution)/shard_map/ppermute | solution.py:368
  68.8 8.7 %copy-start.12 = (f32[7,128,128]{2,1,0:T(8,128)S(1)}, f32[7,128,128]{2,1,0:T(8,128)}, u32[]{:S(2)}) copy-start(f32[7,128,128]{2,1,0:T(8,128)} %copy-done.11) | copy-start | bytes 1376260
  76.9 6.0 %collective-permute-start.23 = (f32[896,256]{1,0:T(8,128)S(1)}, f32[896,256]{1,0:T(8,128)S(1)}, u32[]{:S(2)}, u32[]{:S(2)}) collective-permute-start(f32[896,256]{1,0:T(8,128)S(1)} %get-tuple-element.30), channel_id=1, source_target_pairs={{0,1},{1,0},{2,3},{3,2},{4,5},{5,4},{6,7},{7,6},{8,9},{9,8},{10,11... | collective-permute-start | bytes 2752520 | tf_op jit(solution)/shard_map/ppermute | solution.py:368
  77.4 5.5 %copy-start.8 = (f32[2,128,128]{2,1,0:T(8,128)S(1)}, f32[2,128,128]{2,1,0:T(8,128)}, u32[]{:S(2)}) copy-start(f32[2,128,128]{2,1,0:T(8,128)} %nl_ref.3) | copy-start | bytes 393220
where the time goes:
time: 85.1 us; the launch traced here: 84.7 us
  starting transfers between devices  36.5 us (43%)
  Pallas kernels  32.5 us (38%)
  waiting for transfers between devices  10.2 us (12%)
  local copies, waits for them, and re-layouts  5.3 us (6%)
    ppermute x15, starting transfers between devices, exchange(): return lax.ppermute(block, 'col', route)  23.9 us
    pallas_call x2, Pallas kernels, chain(): pl.pallas_call(functools.partial(chain_kernel, lower), out_shape=(shape,...  13.6 us
    ppermute x9, starting transfers between devices, swap_rows(): return lax.ppermute(block, 'row', [(0, 1), (1, 0)])  12.6 us
    ppermute x15, waiting for transfers between devices, exchange(): return lax.ppermute(block, 'col', route)  6.5 us
    pallas_call x1, Pallas kernels, prepare_cross(): pl.pallas_call(cross_kernel, out_shape=jax.ShapeDtypeStruct((blocks, half...  6.36 us
    pallas_call x1, Pallas kernels, prepare_own(): pl.pallas_call(own_kernel, out_shape=shapes, grid_spec=pltpu.PrefetchScal...  5.61 us
    unnamed x34, local copies, waits for them, and re-layouts  5.29 us
    ppermute x9, waiting for transfers between devices, swap_rows(): return lax.ppermute(block, 'row', [(0, 1), (1, 0)])  3.66 us
  transfers between devices with their start and end apart: 24, of which 6 were waited for; matrix products, arithmetic and copies ran while one was open for 0% of the time, Pallas kernels for 30%

commit v1 on v0

v1 whole, which is shorter than its diff:
```python
import functools

import jax
import jax.numpy as jnp
from jax import lax
from jax.experimental import pallas as pl
from jax.experimental.pallas import tpu as pltpu
from jax.sharding import PartitionSpec as P


F32 = jnp.float32
BF16 = jnp.bfloat16
GRANT = 12 << 20

VMEM = pl.BlockSpec(memory_space=pltpu.VMEM)
SMEM = pl.BlockSpec(memory_space=pltpu.SMEM)
HBM = pl.BlockSpec(memory_space=pltpu.HBM)


def split(x):
    high = x.astype(BF16)
    return high, (x - high.astype(F32)).astype(BF16)


def mm(a, b):
    return jnp.dot(a, b, preferred_element_type=F32)


def cat(parts, axis):
    return jnp.concatenate(parts, axis=axis)


def lhs(x):
    return cat(split(x), 1)


def wide_rhs(x):
    high, low = split(x)
    return cat([high, high], 0), low


def wide_dot(a, b):
    n = a.shape[1] // 2
    return mm(a, b[0]) + mm(a[:, :n], b[1])


def block_rhs(x):
    both = cat(split(x), 1)
    return cat([both, both], 0)


def block_dot(a, b):
    n = b.shape[1] // 2
    r = mm(a, b)
    return r[:, :n] + r[:, n:]


def params(**kw):
    return pltpu.CompilerParams(vmem_limit_bytes=GRANT, **kw)


def place(slots):
    return lax.axis_index("row"), lax.axis_index("col") % slots


def partial_kernel(own, order_hbm, a_hbm, b_hbm, *refs):
    small, refs = (refs[:5], refs[5:]) if not own else ((), refs)
    out_ref, refs = refs[0], refs[1:]
    const_ref, refs = (refs[0], refs[1:]) if not own else (None, refs)
    order, a_buf, b_buf, sems = refs
    slots, depth, _ = out_ref.shape
    groups = order.shape[1]
    size = b_buf.shape[0] // groups
    row, where = place(slots)
    half = 1 - row if own else row
    copies = [
        pltpu.make_async_copy(order_hbm, order, sems.at[slots]),
        pltpu.make_async_copy(b_hbm, b_buf, sems.at[slots + 1]),
    ]
    for m in range(slots):
        rows = pl.multiple_of((half * slots + (where ^ m)) * depth, 8)
        copies.append(
            pltpu.make_async_copy(a_hbm.at[pl.ds(rows, depth)], a_buf.at[m], sems.at[m])
        )
    if not own:
        _, _, _, av, bv = small
        targets = (
            const_ref.at[pl.ds(0, 2)],
            const_ref.at[pl.ds(2, 2)],
            const_ref.at[4],
            const_ref.at[5, pl.ds(0, av.shape[0])],
            const_ref.at[6, pl.ds(0, bv.shape[0])],
        )
        for j, (source, target) in enumerate(zip(small, targets)):
            copies.append(pltpu.make_async_copy(source, target, sems.at[slots + 2 + j]))
    for copy in copies:
        copy.start()
    copies[0].wait()
    copies[1].wait()
    paired = [
        b_buf[pl.ds(pl.multiple_of(order[0, g] * size, size), size), :]
        for g in range(groups)
    ]
    high, low = split(cat(paired, 0))
    for m in range(slots):
        copies[2 + m].wait()
        ah, al = split(a_buf[m])
        out_ref[m] = mm(ah, high) + (mm(ah, low) + mm(al, high))
    for copy in copies[2 + slots :]:
        copy.wait()


def partial_product(order, top_rows, lower, slots, small=None):
    own = small is None
    depth, inner = top_rows.shape[0] // 2 // slots, top_rows.shape[1]
    out = jax.ShapeDtypeStruct((slots, depth, lower.shape[1]), F32)
    operands = (order, top_rows, lower) + (() if own else small)
    if not own:
        out = (out, jax.ShapeDtypeStruct((7,) + small[2].shape, F32))
    return pl.pallas_call(
        functools.partial(partial_kernel, own),
        out_shape=out,
        in_specs=[HBM] * len(operands),
        out_specs=VMEM if own else (VMEM, VMEM),
        scratch_shapes=[
            pltpu.SMEM(order.shape, jnp.int32),
            pltpu.VMEM((slots, depth, inner), F32),
            pltpu.VMEM(lower.shape, F32),
            pltpu.SemaphoreType.DMA((slots + 7,)),
        ],
        compiler_params=params(),
        name="partial_own" if own else "partial_other",
    )(*operands)


def add_kernel(slots, a_ref, b_ref, *outs):
    for m in range(slots):
        outs[m][...] = a_ref[m] + b_ref[m]


def add_slots(a, b):
    slots = a.shape[0]
    shape = pltpu.VMEM(a.shape[1:], F32)
    return pl.pallas_call(
        functools.partial(add_kernel, slots),
        out_shape=(shape,) * slots,
        in_specs=[VMEM, VMEM],
        out_specs=(VMEM,) * slots,
        compiler_params=params(),
        name="add_slots",
    )(a, b)


def sum_kernel(*refs):
    total = refs[0][...]
    for r in refs[1:-1]:
        total = total + r[...]
    refs[-1][...] = total


def sum_slots(*parts):
    return pl.pallas_call(
        sum_kernel,
        out_shape=jax.ShapeDtypeStruct(parts[0].shape, F32),
        in_specs=[VMEM] * len(parts),
        out_specs=VMEM,
        compiler_params=params(),
        name="sum_slots",
    )(*parts)


def side_kernel(*refs):
    goal, const, out = refs[-3:]
    total = refs[0][...]
    for r in refs[1:-3]:
        total = total + r[...]
    side = goal[...] - total
    n = const.shape[1]
    for c in range(2):
        cols = slice(c * n, (c + 1) * n)
        out[:, cols] = block_dot(lhs(side[:, cols]), block_rhs(const[c]))


def side_slot(parts, goal, const):
    return pl.pallas_call(
        side_kernel,
        out_shape=jax.ShapeDtypeStruct(goal.shape, F32),
        in_specs=[VMEM] * (len(parts) + 2),
        out_specs=VMEM,
        compiler_params=params(),
        name="side_slot",
    )(*parts, goal, const)


def stage_kernel(*refs):
    count = len(refs) // 2
    sems = refs[-1]
    copies = [
        pltpu.make_async_copy(refs[j], refs[count + j], sems.at[j]) for j in range(count)
    ]
    for copy in copies:
        copy.start()
    for copy in copies:
        copy.wait()


def stage(*arrays):
    return pl.pallas_call(
        stage_kernel,
        out_shape=tuple(jax.ShapeDtypeStruct(a.shape, F32) for a in arrays),
        in_specs=[HBM] * len(arrays),
        out_specs=(VMEM,) * len(arrays),
        scratch_shapes=[pltpu.SemaphoreType.DMA((len(arrays),))],
        compiler_params=params(),
        name="stage",
    )(*arrays)


def rotate_kernel(slots, *refs):
    rs, (q_ref, out, buf) = refs[:slots], refs[slots:]
    blocks, n, _ = q_ref.shape
    _, where = place(slots)
    for m in range(slots):
        depth = rs[m].shape[0]
        buf[pl.ds(pl.multiple_of((where ^ m) * depth, 8), depth), :] = rs[m][...]
    for i in range(blocks):
        rows = slice(i * n, (i + 1) * n)
        out[rows, :] = wide_dot(lhs(q_ref[i]), wide_rhs(buf[rows, :]))


def rotate(parts, q):
    blocks, n, _ = q.shape
    shape = (blocks * n, parts[0].shape[1])
    return pl.pallas_call(
        functools.partial(rotate_kernel, len(parts)),
        out_shape=jax.ShapeDtypeStruct(shape, F32),
        in_specs=[VMEM] * (len(parts) + 1),
        out_specs=VMEM,
        scratch_shapes=[pltpu.VMEM(shape, F32)],
        compiler_params=params(),
        name="rotate",
    )(*parts, q)


def first_block(k):
    return k * (k - 1) // 2


def prepare_kernel(u_hbm, q_hbm, p_hbm, const, out_ref, u_buf, q_buf, p_buf, sems):
    blocks, n, _ = p_buf.shape
    row = lax.axis_index("row")
    base = first_block(blocks)
    copies = [
        pltpu.make_async_copy(q_hbm, q_buf, sems.at[blocks]),
        pltpu.make_async_copy(p_hbm, p_buf, sems.at[blocks + 1]),
    ]
    for i in range(blocks - 1):
        first, count = (i + 1) * n, (blocks - 1 - i) * n
        cols = pl.multiple_of(row * (blocks * n) + first, n)
        copies.append(
            pltpu.make_async_copy(
                u_hbm.at[pl.ds(i * n, n), pl.ds(cols, count)],
                u_buf.at[pl.ds(i * n, n), pl.ds(first, count)],
                sems.at[i],
            )
        )
    for copy in copies:
        copy.start()
    left = lhs(const[2])
    out_ref[base + 2 * blocks] = block_dot(left, block_rhs(const[0]))
    both = block_dot(left, block_rhs(const[4]))
    out_ref[base + 2 * blocks + 1] = block_dot(lhs(both), block_rhs(const[1]))
    out_ref[base + 2 * blocks + 2] = block_dot(lhs(const[3]), block_rhs(const[1]))
    out_ref[base + 2 * blocks + 3, :blocks] = const[5, :blocks]
    for copy in copies[:2]:
        copy.wait()
    p = [block_rhs(p_buf[k]) for k in range(blocks)]
    out_ref[base + blocks : base + 2 * blocks] = p_buf[...]
    for i in range(blocks):
        q = lhs(q_buf[i])
        out_ref[base + i] = block_dot(q, p[i])
        if i + 1 == blocks:
            break
        copies[2 + i].wait()
        qu = wide_dot(q, wide_rhs(u_buf[i * n : (i + 1) * n, (i + 1) * n :]))
        for k in range(i + 1, blocks):
            own = qu[:, (k - i - 1) * n : (k - i) * n]
            out_ref[first_block(k) + i] = block_dot(lhs(own), p[k])


def prepare(corner, q, p, const):
    blocks, n, _ = q.shape
    count = first_block(blocks) + 2 * blocks + 4
    return pl.pallas_call(
        prepare_kernel,
        out_shape=jax.ShapeDtypeStruct((count, n, n), F32),
        in_specs=[HBM, HBM, HBM, VMEM],
        out_specs=VMEM,
        scratch_shapes=[
            pltpu.VMEM((blocks * n, blocks * n), F32),
            pltpu.VMEM(q.shape, F32),
            pltpu.VMEM(p.shape, F32),
            pltpu.SemaphoreType.DMA((blocks + 2,)),
        ],
        compiler_params=params(),
        name="prepare",
    )(corner, q, p, const)


def cross_kernel(first, u_hbm, q_hbm, t_hbm, out_ref, u_buf, q_buf, p_buf, sems):
    blocks, n, _ = p_buf.shape
    count = q_buf.shape[0]
    base = first_block(blocks) + blocks

    @pl.when(lax.axis_index("row") == 0)
    def _():
        copies = [
            pltpu.make_async_copy(
                t_hbm.at[pl.ds(base, blocks)], p_buf, sems.at[count]
            ),
            pltpu.make_async_copy(q_hbm.at[pl.ds(first, count)], q_buf, sems.at[count + 1]),
        ]
        for i in range(count):
            copies.append(
                pltpu.make_async_copy(
                    u_hbm.at[pl.ds((first + i) * n, n), pl.ds(blocks * n, blocks * n)],
                    u_buf.at[pl.ds(i * n, n)],
                    sems.at[i],
                )
            )
        for copy in copies:
            copy.start()
        for copy in copies[:2]:
            copy.wait()
        p = [block_rhs(p_buf[k]) for k in range(blocks)]
        for i in range(count):
            copies[2 + i].wait()
            rows = slice(i * n, (i + 1) * n)
            qu = wide_dot(lhs(q_buf[i]), wide_rhs(u_buf[rows, :]))
            for k in range(blocks):
                own = lhs(qu[:, k * n : (k + 1) * n])
                out_ref[k, rows, :] = lhs(block_dot(own, p[k]))


def prepare_cross(first, last, corner, q, shipped):
    blocks, n, _ = q.shape
    count = last - first
    return pl.pallas_call(
        functools.partial(cross_kernel, first),
        out_shape=jax.ShapeDtypeStruct((blocks, count * n, 2 * n), BF16),
        in_specs=[HBM, HBM, HBM],
        out_specs=VMEM,
        scratch_shapes=[
            pltpu.VMEM((count * n, blocks * n), F32),
            pltpu.VMEM((count,) + q.shape[1:], F32),
            pltpu.VMEM(q.shape, F32),
            pltpu.SemaphoreType.DMA((count + 2,)),
        ],
        compiler_params=params(),
    )(corner, q, shipped)


def chain_kernel(lower, *refs):
    if lower:
        c_ref, t_ref, const, z_ref, h_ref, c_buf = refs
    else:
        c_ref, w_ref, t_ref, const, z_ref, c_buf = refs
    row = lax.axis_index("row")
    n = t_ref.shape[1]
    blocks = c_ref.shape[0] // n
    base = first_block(blocks)
    left = slice(0, n)
    right = slice(n, 2 * n)

    def rows(i):
        return slice(i * n, (i + 1) * n)

    @pl.when(row == 0)
    def _():
        bv = const[6, :8]
        gs = [t_ref[base + 2 * blocks + j] for j in range(3)]
        g0 = wide_rhs(cat(gs[:2], 1))
        g1 = block_rhs(gs[2])
        av = t_ref[base + 2 * blocks + 3, : 8 * ((blocks + 7) // 8), :]

        def inverse(i, c):
            own = jnp.transpose(jnp.broadcast_to(av[i : i + 1, :], (n, n)))
            return 1.0 / (own + jnp.broadcast_to(bv[c : c + 1, :], (n, n)))

        if lower:
            c_buf[...] = c_ref[...]
        else:
            c_buf[...] = c_ref[...] - w_ref[...]
        for i in range(blocks - 1, -1, -1):
            z0 = c_buf[rows(i), left] * inverse(i, 0)
            z_ref[rows(i), left] = z0
            hj = wide_dot(lhs(z0), g0)
            h0 = hj[:, left]
            if i > 0:
                t = lhs(t_ref[first_block(i) + i - 1])
                c_buf[rows(i - 1), left] -= block_dot(t, block_rhs(h0))
            coupled = block_dot(lhs(t_ref[base + i]), block_rhs(hj[:, right]))
            z1 = (c_buf[rows(i), right] - coupled) * inverse(i, 1)
            z_ref[rows(i), right] = z1
            if lower or i > 0:
                h1 = block_dot(lhs(z1), g1)
            if i > 0:
                c_buf[rows(i - 1), right] -= block_dot(t, block_rhs(h1))
            if lower:
                h_ref[rows(i), left] = h0
                h_ref[rows(i), right] = h1
            if i > 1:
                h = wide_rhs(cat([h0, h1], 1))
                above = t_ref[first_block(i) : first_block(i) + i - 1]
                above = lhs(above.reshape((i - 1) * n, n))
                c_buf[: (i - 1) * n, :] -= wide_dot(above, h)

    if lower:

        @pl.when(row != 0)
        def _():
            z_ref[...] = c_ref[...]


def chain(c, w, t, const):
    lower = w is None
    shape = jax.ShapeDtypeStruct(c.shape, F32)
    operands = [c] + ([] if lower else [w]) + [t, const]
    return pl.pallas_call(
        functools.partial(chain_kernel, lower),
        out_shape=(shape, shape) if lower else shape,
        in_specs=[VMEM] * len(operands),
        out_specs=(VMEM, VMEM) if lower else VMEM,
        scratch_shapes=[pltpu.VMEM(shape.shape, F32)],
        compiler_params=params(),
        name="chain_lower" if lower else "chain_upper",
    )(*operands)


def apply_kernel(*refs):
    toffs, (h_ref, w_ref) = refs[:-2], refs[-2:]
    blocks, _, wide = toffs[0].shape
    n = wide // 2

    @pl.when(lax.axis_index("row") == 0)
    def _():
        hs = [wide_rhs(h_ref[k * n : (k + 1) * n, :]) for k in range(blocks)]
        first = 0
        for toff in toffs:
            total = wide_dot(toff[0], hs[0])
            for k in range(1, blocks):
                total = total + wide_dot(toff[k], hs[k])
            w_ref[first : first + toff.shape[1], :] = total
            first += toff.shape[1]


def apply_cross(toffs, h):
    return pl.pallas_call(
        apply_kernel,
        out_shape=jax.ShapeDtypeStruct(h.shape, F32),
        in_specs=[VMEM] * (len(toffs) + 1),
        out_specs=VMEM,
        compiler_params=params(),
        name="apply_cross",
    )(*toffs, h)


def final_kernel(upper_ref, lower_ref, t_ref, const, out_ref):
    n = t_ref.shape[1]
    blocks = out_ref.shape[0] // n
    base = first_block(blocks) + blocks
    nl = [block_rhs(const[2 + c]) for c in range(2)]

    def solve(z_ref):
        for i in range(blocks):
            rows = slice(i * n, (i + 1) * n)
            y = [
                block_dot(lhs(z_ref[rows, c * n : (c + 1) * n]), nl[c]) for c in range(2)
            ]
            out_ref[rows, :] = wide_dot(lhs(t_ref[base + i]), wide_rhs(cat(y, 1)))

    @pl.when(lax.axis_index("row") == 0)
    def _():
        solve(upper_ref)

    @pl.when(lax.axis_index("row") != 0)
    def _():
        solve(lower_ref)


def final(z_upper, z_lower, packed, const):
    return pl.pallas_call(
        final_kernel,
        out_shape=jax.ShapeDtypeStruct(z_upper.shape, F32),
        in_specs=[VMEM] * 4,
        out_specs=VMEM,
        compiler_params=params(),
        name="final",
    )(z_upper, z_lower, packed, const)


def exchange(block, mask):
    route = [(i, i ^ mask) for i in range(lax.axis_size("col"))]
    return lax.ppermute(block, "col", route)


def swap_rows(block):
    return lax.ppermute(block, "row", [(0, 1), (1, 0)])


def far(x):
    return pltpu.with_memory_space_constraint(x, pltpu.HBM)


def body(
    top_rows, lower_new, block_order, corner, target, coupling,
    top_right, top_left, top_values, new_right, new_left, new_values,
):
    cols = lax.axis_size("col")
    half_rows = target.shape[0]
    slots = min(cols, 8)
    depth = half_rows // slots
    where = lax.axis_index("col") % slots
    small = (new_right, new_left, coupling, top_values, new_values)
    small = tuple(map(far, small))
    block_order, top_rows, lower_new, corner, top_left, top_right = map(
        far, (block_order, top_rows, lower_new, corner, top_left, top_right)
    )

    theirs, const = partial_product(block_order, top_rows, lower_new, slots, small)
    theirs = swap_rows(theirs)
    ours = partial_product(block_order, top_rows, lower_new, slots)
    q_other = far(swap_rows(top_left))
    goal = swap_rows(lax.dynamic_slice_in_dim(target, where * depth, depth, 0))
    pieces = add_slots(ours, theirs)
    received = [exchange(pieces[m], m) for m in range(1, slots)]
    packed = prepare(corner, top_left, top_right, const)
    shipped = far(swap_rows(packed))
    blocks = top_left.shape[0]
    cut = blocks * 3 // 7
    toffs = (
        prepare_cross(0, cut, corner, top_left, shipped),
        prepare_cross(cut, blocks, corner, top_left, shipped),
    )
    near, q_near = stage(shipped, q_other)

    total = sum_slots(pieces[0], *received)
    mask = slots
    last = []
    while mask < cols:
        moved = exchange(total, mask)
        if mask * 2 < cols:
            total = total + moved
        else:
            last = [moved]
        mask *= 2
    side = side_slot([total] + last, goal, const)
    parts = [side] + [exchange(side, m) for m in range(1, slots)]
    c_own = rotate(parts, q_near)
    z_lower, h = chain(c_own, None, near, const)
    moved = swap_rows(z_lower)
    w = apply_cross(toffs, h)
    z_upper = chain(moved, w, packed, const)
    return final(z_upper, moved, packed, const)


def solution(mesh):
    placed = (
        P(None, ("col", "row")),
        P(("col", "row"), None),
        P(("col", "row"), None),
        P("row", None),
        P("row", None),
        P(),
        P("row", None, None),
        P("row", None, None),
        P("row", None),
        P(),
        P(),
        P(),
    )
    return jax.shard_map(
        body, mesh=mesh, in_specs=placed, out_specs=P("row", None), check_vma=False
    )
```

time: 85.1 us -> 84.7 us (level)
  the two profiles are of different devices: /device:TPU:1 before, /device:TPU:0 now
where the time goes in v1:
time: 84.7 us; the launch traced here: 84.4 us
  Pallas kernels  31.9 us (38%)
  starting transfers between devices  23.9 us (28%)
  waiting for transfers between devices  22.4 us (26%)
  local copies, waits for them, and re-layouts  6.06 us (7%)
    ppermute x15, starting transfers between devices, exchange(): return lax.ppermute(block, 'col', route)  23.2 us
    ppermute x15, waiting for transfers between devices, exchange(): return lax.ppermute(block, 'col', route)  19.8 us
    pallas_call x2, Pallas kernels, chain(): pl.pallas_call(functools.partial(chain_kernel, lower), out_shape=(shape,...  7.21 us
    pallas_call x2, Pallas kernels, partial_product(): pl.pallas_call(functools.partial(partial_kernel, own), out_shape=out, in_...  6.26 us
    pallas_call x2, Pallas kernels, prepare_cross(): pl.pallas_call(functools.partial(cross_kernel, first), out_shape=jax.Shap...  6.2 us
    unnamed x22, local copies, waits for them, and re-layouts  6.05 us
    pallas_call x1, Pallas kernels, prepare(): pl.pallas_call(prepare_kernel, out_shape=jax.ShapeDtypeStruct((count, n,...  4.12 us
    ppermute x5, waiting for transfers between devices, swap_rows(): return lax.ppermute(block, 'row', [(0, 1), (1, 0)])  2.59 us
  transfers between devices with their start and end apart: 20, of which 10 were waited for; matrix products, arithmetic and copies ran while one was open for 0% of the time, Pallas kernels for 18%

profile of v1, /device:TPU:0, one launch (start us, length us, event | category | flops | bytes accessed | tf_op | source)
XLA Modules:
  0.0 84.4 jit_solution(13169115581994390389)
XLA Ops:
  0.0 3.2 %partial_other.1 = (f32[8,112,256]{2,1,0:T(8,128)S(1)}, f32[7,128,128]{2,1,0:T(8,128)S(1)}) custom-call(s32[1,2]{1,0:T(1,128)} %order_hbm.3, f32[1792,256]{1,0:T(8,128)} %a_hbm.3, f32[256,256]{1,0:T(8,128)} %b_hbm.3, f32[2,128,128]{2,1,0:T(8,128)} %refs_0_.1, f32[2,128,128]{2,1,0:T(8,128)} %refs_1_.1, f32[128,128]{1,0:T(8,128)} %refs_2_.1, ...), custom_call_target="tpu_custom_call" | custom-call | tf_op jit(solution)/shard_map/partial_other/pallas_call | solution.py:120
  3.2 4.1 %prepare.1.refs_2_.t_ref = f32[39,128,128]{2,1,0:T(8,128)S(1)} custom-call(f32[896,1792]{1,0:T(8,128)} %u_hbm.5, f32[7,128,128]{2,1,0:T(8,128)} %q_hbm.5, f32[7,128,128]{2,1,0:T(8,128)} %p_hbm.1, f32[7,128,128]{2,1,0:T(8,128)S(1)} %get-tuple-element.28.refs_3_.const.refs_2_), custom_call_target="tpu_custom_call" | custom-call | tf_op jit(solution)/shard_map/prepare/pallas_call | solution.py:294
  7.3 0.6 collective-permute-start.17
  7.9 0.1 collective-permute-start
  8.0 3.1 %partial_own.1.a_ref = f32[8,112,256]{2,1,0:T(8,128)S(1)} custom-call(s32[1,2]{1,0:T(1,128)} %order_hbm.3, f32[1792,256]{1,0:T(8,128)} %a_hbm.3, f32[256,256]{1,0:T(8,128)} %b_hbm.3), custom_call_target="tpu_custom_call" | custom-call | tf_op jit(solution)/shard_map/partial_own/pallas_call | solution.py:120
  11.1 2.6 %collective-permute-done.b_ref = f32[8,112,256]{2,1,0:T(8,128)S(1)} collective-permute-done((f32[8,112,256]{2,1,0:T(8,128)S(1)}, f32[8,112,256]{2,1,0:T(8,128)S(1)}, u32[]{:S(2)}, u32[]{:S(2)}) %collective-permute-start) | collective-permute-done | bytes 917536 | tf_op jit(solution)/shard_map/ppermute | solution.py:508
  13.6 0.8 add_slots.1
  14.4 0.6 copy-done.4
  15.1 0.6 copy-done.8
  15.7 0.6 copy-done.9
  16.4 0.6 copy-done.10
  17.0 2.8 %collective-permute-start.1 = (f32[112,256]{1,0:T(8,128)S(1)}, f32[112,256]{1,0:T(8,128)S(1)}, u32[]{:S(2)}, u32[]{:S(2)}) collective-permute-start(f32[112,256]{1,0:T(8,128)S(1)} %get-tuple-element.21), channel_id=1, source_target_pairs={{0,2},{2,0},{4,6},{6,4},{8,10},{10,8},{12,14},{14,12},{16,18},{18,... | collective-permute-start | bytes 344072 | tf_op jit(solution)/shard_map/ppermute | solution.py:504
  19.9 1.5 %collective-permute-start.2 = (f32[112,256]{1,0:T(8,128)}, f32[112,256]{1,0:T(8,128)}, u32[]{:S(2)}, u32[]{:S(2)}) collective-permute-start(f32[112,256]{1,0:T(8,128)} %get-tuple-element.22), channel_id=1, source_target_pairs={{0,4},{2,6},{4,0},{6,2},{8,12},{10,14},{12,8},{14,10},{16,20},{18,... | collective-permute-start | bytes 344072 | tf_op jit(solution)/shard_map/ppermute | solution.py:504
  21.4 2.0 %collective-permute-start.4 = (f32[112,256]{1,0:T(8,128)}, f32[112,256]{1,0:T(8,128)}, u32[]{:S(2)}, u32[]{:S(2)}) collective-permute-start(f32[112,256]{1,0:T(8,128)} %get-tuple-element.24), channel_id=1, source_target_pairs={{0,8},{2,10},{4,12},{6,14},{8,0},{10,2},{12,4},{14,6},{16,24},{18,... | collective-permute-start | bytes 344072 | tf_op jit(solution)/shard_map/ppermute | solution.py:504
  23.4 0.6 copy-done.6
  24.1 3.5 %collective-permute-done.2.refs_2_ = f32[112,256]{1,0:T(8,128)} collective-permute-done((f32[112,256]{1,0:T(8,128)}, f32[112,256]{1,0:T(8,128)}, u32[]{:S(2)}, u32[]{:S(2)}) %collective-permute-start.2) | collective-permute-done | bytes 114720 | tf_op jit(solution)/shard_map/ppermute | solution.py:504
  27.5 0.6 collective-permute-start.5
  28.2 2.3 %collective-permute-start.6 = (f32[112,256]{1,0:T(8,128)}, f32[112,256]{1,0:T(8,128)S(1)}, u32[]{:S(2)}, u32[]{:S(2)}) collective-permute-start(f32[112,256]{1,0:T(8,128)} %copy-done.9), channel_id=1, source_target_pairs={{0,12},{2,14},{4,8},{6,10},{8,4},{10,6},{12,0},{14,2},{16,28},{18,... | collective-permute-start | bytes 344072 | tf_op jit(solution)/shard_map/ppermute | solution.py:504
  30.5 2.4 %collective-permute-start.7 = (f32[112,256]{1,0:T(8,128)}, f32[112,256]{1,0:T(8,128)S(1)}, u32[]{:S(2)}, u32[]{:S(2)}) collective-permute-start(f32[112,256]{1,0:T(8,128)} %copy-done.8), channel_id=1, source_target_pairs={{0,14},{2,12},{4,10},{6,8},{8,6},{10,4},{12,2},{14,0},{16,30},{18,... | collective-permute-start | bytes 344072 | tf_op jit(solution)/shard_map/ppermute | solution.py:504
  33.0 1.4 %collective-permute-done.5.refs_5_ = f32[112,256]{1,0:T(8,128)S(1)} collective-permute-done((f32[112,256]{1,0:T(8,128)}, f32[112,256]{1,0:T(8,128)S(1)}, u32[]{:S(2)}, u32[]{:S(2)}) %collective-permute-start.5) | collective-permute-done | bytes 114720 | tf_op jit(solution)/shard_map/ppermute | solution.py:504
  34.4 2.1 %collective-permute-done.6.refs_6_ = f32[112,256]{1,0:T(8,128)S(1)} collective-permute-done((f32[112,256]{1,0:T(8,128)}, f32[112,256]{1,0:T(8,128)S(1)}, u32[]{:S(2)}, u32[]{:S(2)}) %collective-permute-start.6) | collective-permute-done | bytes 114720 | tf_op jit(solution)/shard_map/ppermute | solution.py:504
  36.5 2.0 %collective-permute-done.7.refs_7_ = f32[112,256]{1,0:T(8,128)S(1)} collective-permute-done((f32[112,256]{1,0:T(8,128)}, f32[112,256]{1,0:T(8,128)S(1)}, u32[]{:S(2)}, u32[]{:S(2)}) %collective-permute-start.7) | collective-permute-done | bytes 114720 | tf_op jit(solution)/shard_map/ppermute | solution.py:504
  38.6 0.9 %copy-done.5 = f32[112,256]{1,0:T(8,128)S(1)} copy-done((f32[112,256]{1,0:T(8,128)S(1)}, f32[112,256]{1,0:T(8,128)}, u32[]{:S(2)}) %copy-start.5) | copy-done | bytes 114712
  39.5 0.9 %copy-done.7 = f32[112,256]{1,0:T(8,128)S(1)} copy-done((f32[112,256]{1,0:T(8,128)S(1)}, f32[112,256]{1,0:T(8,128)}, u32[]{:S(2)}) %copy-start.7) | copy-done | bytes 114712
  40.4 1.1 %sum_slots.1.refs_0_ = f32[112,256]{1,0:T(8,128)S(1)} custom-call(f32[112,256]{1,0:T(8,128)S(1)} %copy-done.5, f32[112,256]{1,0:T(8,128)S(1)} %copy-done.7, f32[112,256]{1,0:T(8,128)} %collective-permute-done.2.refs_2_, f32[112,256]{1,0:T(8,128)} %collective-permute-done.3.refs_3_, f32[112,256]{1,0:T(8,128)} %collective-permute-done.4.refs_4_, ...), custom_call_target="tpu_custom_call" | custom-call | tf_op jit(solution)/shard_map/sum_slots/pallas_call | solution.py:162
  41.4 2.6 %collective-permute-start.8 = (f32[112,256]{1,0:T(8,128)S(1)}, f32[112,256]{1,0:T(8,128)S(1)}, u32[]{:S(2)}, u32[]{:S(2)}) collective-permute-start(f32[112,256]{1,0:T(8,128)S(1)} %sum_slots.1.refs_0_), channel_id=1, source_target_pairs={{0,16},{2,18},{4,20},{6,22},{8,24},{10,26},{12,28},{14,30},{16,0},... | collective-permute-start | bytes 344072 | tf_op jit(solution)/shard_map/ppermute | solution.py:504
  44.1 4.3 %collective-permute-done.8.refs_1_ = f32[112,256]{1,0:T(8,128)S(1)} collective-permute-done((f32[112,256]{1,0:T(8,128)S(1)}, f32[112,256]{1,0:T(8,128)S(1)}, u32[]{:S(2)}, u32[]{:S(2)}) %collective-permute-start.8) | collective-permute-done | bytes 114720 | tf_op jit(solution)/shard_map/ppermute | solution.py:504
  48.4 1.0 %copy-done.2 = f32[7,128,128]{2,1,0:T(8,128)S(1)} copy-done((f32[7,128,128]{2,1,0:T(8,128)S(1)}, f32[7,128,128]{2,1,0:T(8,128)}, u32[]{:S(2)}) %copy-start.2) | copy-done | bytes 458776
  49.4 0.2 side_slot.1.refs_0_
  49.6 0.8 collective-permute-start.10
  50.4 1.0 %collective-permute-start.11 = (f32[112,256]{1,0:T(8,128)S(1)}, f32[112,256]{1,0:T(8,128)S(1)}, u32[]{:S(2)}, u32[]{:S(2)}) collective-permute-start(f32[112,256]{1,0:T(8,128)S(1)} %side_slot.1.refs_0_), channel_id=1, source_target_pairs={{0,4},{2,6},{4,0},{6,2},{8,12},{10,14},{12,8},{14,10},{16,20},{18,... | collective-permute-start | bytes 344072 | tf_op jit(solution)/shard_map/ppermute | solution.py:504
  51.4 1.8 %collective-permute-start.12 = (f32[112,256]{1,0:T(8,128)S(1)}, f32[112,256]{1,0:T(8,128)S(1)}, u32[]{:S(2)}, u32[]{:S(2)}) collective-permute-start(f32[112,256]{1,0:T(8,128)S(1)} %side_slot.1.refs_0_), channel_id=1, source_target_pairs={{0,6},{2,4},{4,2},{6,0},{8,14},{10,12},{12,10},{14,8},{16,22},{18,... | collective-permute-start | bytes 344072 | tf_op jit(solution)/shard_map/ppermute | solution.py:504
  53.2 0.7 collective-permute-start.13
  53.9 1.9 %collective-permute-done.10.refs_1_ = f32[112,256]{1,0:T(8,128)S(1)} collective-permute-done((f32[112,256]{1,0:T(8,128)S(1)}, f32[112,256]{1,0:T(8,128)S(1)}, u32[]{:S(2)}, u32[]{:S(2)}) %collective-permute-start.10) | collective-permute-done | bytes 114720 | tf_op jit(solution)/shard_map/ppermute | solution.py:504
  55.7 0.8 collective-permute-start.14
  56.6 2.4 %collective-permute-done.11.refs_2_ = f32[112,256]{1,0:T(8,128)S(1)} collective-permute-done((f32[112,256]{1,0:T(8,128)S(1)}, f32[112,256]{1,0:T(8,128)S(1)}, u32[]{:S(2)}, u32[]{:S(2)}) %collective-permute-start.11) | collective-permute-done | bytes 114720 | tf_op jit(solution)/shard_map/ppermute | solution.py:504
  58.9 3.7 %collective-permute-start.16 = (f32[112,256]{1,0:T(8,128)S(1)}, f32[112,256]{1,0:T(8,128)S(1)}, u32[]{:S(2)}, u32[]{:S(2)}) collective-permute-start(f32[112,256]{1,0:T(8,128)S(1)} %side_slot.1.refs_0_), channel_id=1, source_target_pairs={{0,14},{2,12},{4,10},{6,8},{8,6},{10,4},{12,2},{14,0},{16,30},{18,... | collective-permute-start | bytes 344072 | tf_op jit(solution)/shard_map/ppermute | solution.py:504
  62.6 1.8 %stage.1 = (f32[39,128,128]{2,1,0:T(8,128)S(1)}, f32[7,128,128]{2,1,0:T(8,128)S(1)}) custom-call(f32[39,128,128]{2,1,0:T(8,128)} %collective-permute-done.17.refs_0_.t_hbm, f32[7,128,128]{2,1,0:T(8,128)} %collective-permute-done.18.refs_1_), custom_call_target="tpu_custom_call" | custom-call | tf_op jit(solution)/shard_map/stage/pallas_call | solution.py:208
  64.4 0.2 collective-permute-done.15.refs_6_
  64.6 2.0 %collective-permute-done.16.refs_7_ = f32[112,256]{1,0:T(8,128)S(1)} collective-permute-done((f32[112,256]{1,0:T(8,128)S(1)}, f32[112,256]{1,0:T(8,128)S(1)}, u32[]{:S(2)}, u32[]{:S(2)}) %collective-permute-start.16) | collective-permute-done | bytes 114720 | tf_op jit(solution)/shard_map/ppermute | solution.py:504
  66.6 0.5 rotate.1.refs_0_
  67.1 3.7 %chain_lower.1 = (f32[896,256]{1,0:T(8,128)S(1)}, f32[896,256]{1,0:T(8,128)S(1)}) custom-call(f32[896,256]{1,0:T(8,128)S(1)} %rotate.1.refs_0_, f32[39,128,128]{2,1,0:T(8,128)S(1)} %get-tuple-element.30.refs_1_, f32[7,128,128]{2,1,0:T(8,128)S(1)} %copy-done.3), custom_call_target="tpu_custom_call" | custom-call | tf_op jit(solution)/shard_map/chain_lower/pallas_call | solution.py:429
  70.7 0.1 collective-permute-start.19
  70.8 3.4 %shard_map.119.refs_1_ = bf16[7,512,256]{2,1,0:T(8,128)(2,1)S(1)} custom-call(f32[896,1792]{1,0:T(8,128)} %u_hbm.5, f32[7,128,128]{2,1,0:T(8,128)} %q_hbm.5, f32[39,128,128]{2,1,0:T(8,128)} %collective-permute-done.17.refs_0_.t_hbm), custom_call_target="tpu_custom_call" | custom-call | tf_op jit(solution)/shard_map/pallas_call | solution.py:348
  74.2 2.8 %shard_map.118.refs_0_ = bf16[7,384,256]{2,1,0:T(8,128)(2,1)S(1)} custom-call(f32[896,1792]{1,0:T(8,128)} %u_hbm.5, f32[7,128,128]{2,1,0:T(8,128)} %q_hbm.5, f32[39,128,128]{2,1,0:T(8,128)} %collective-permute-done.17.refs_0_.t_hbm), custom_call_target="tpu_custom_call" | custom-call | tf_op jit(solution)/shard_map/pallas_call | solution.py:348
  77.0 2.0 %apply_cross.1.refs_1_ = f32[896,256]{1,0:T(8,128)S(1)} custom-call(bf16[7,384,256]{2,1,0:T(8,128)(2,1)S(1)} %shard_map.118.refs_0_, bf16[7,512,256]{2,1,0:T(8,128)(2,1)S(1)} %shard_map.119.refs_1_, f32[896,256]{1,0:T(8,128)S(1)} %get-tuple-element.32.refs_2_), custom_call_target="tpu_custom_call" | custom-call | tf_op jit(solution)/shard_map/apply_cross/pallas_call | solution.py:458
  79.1 3.5 %chain_upper.1.upper_ref = f32[896,256]{1,0:T(8,128)S(1)} custom-call(f32[896,256]{1,0:T(8,128)S(1)} %collective-permute-done.19.refs_0_.lower_ref, f32[896,256]{1,0:T(8,128)S(1)} %apply_cross.1.refs_1_, f32[39,128,128]{2,1,0:T(8,128)S(1)} %prepare.1.refs_2_.t_ref, f32[7,128,128]{2,1,0:T(8,128)S(1)} %copy-done.3), custom_call_target="tpu_custom_call" | custom-call | tf_op jit(solution)/shard_map/chain_upper/pallas_call | solution.py:429
  82.6 1.8 %final.1 = f32[896,256]{1,0:T(8,128)} custom-call(f32[896,256]{1,0:T(8,128)S(1)} %chain_upper.1.upper_ref, f32[896,256]{1,0:T(8,128)S(1)} %collective-permute-done.19.refs_0_.lower_ref, f32[39,128,128]{2,1,0:T(8,128)S(1)} %prepare.1.refs_2_.t_ref, f32[7,128,128]{2,1,0:T(8,128)S(1)} %copy-done.3), custom_call_target="tpu_custom_call" | custom-call | tf_op jit(solution)/shard_map/final/pallas_call | solution.py:492
  (29 shorter events, 0.1 us)
Async XLA Ops:
  0.0 32.9 %copy-start = (f32[896,256]{1,0:T(8,128)S(1)}, f32[896,256]{1,0:T(8,128)}, u32[]{:S(2)}) copy-start(f32[896,256]{1,0:T(8,128)} %param.16) | copy-start | bytes 2752516
  3.2 4.1 %copy-start.1 = (f32[7,128,128]{2,1,0:T(8,128)}, f32[7,128,128]{2,1,0:T(8,128)S(1)}, u32[]{:S(2)}) copy-start(f32[7,128,128]{2,1,0:T(8,128)S(1)} %get-tuple-element.28.refs_3_.const.refs_2_) | copy-start | bytes 1376260
  7.3 51.6 %collective-permute-start.17 = (f32[39,128,128]{2,1,0:T(8,128)S(1)}, f32[39,128,128]{2,1,0:T(8,128)}, u32[]{:S(2)}, u32[]{:S(2)}) collective-permute-start(f32[39,128,128]{2,1,0:T(8,128)S(1)} %prepare.1.refs_2_.t_ref), channel_id=1, source_target_pairs={{0,1},{1,0},{2,3},{3,2},{4,5},{5,4},{6,7},{7,6},{8,9},{9,8},{10,11... | collective-permute-start | bytes 7667720 | tf_op jit(solution)/shard_map/ppermute | solution.py:508
  7.9 5.8 %collective-permute-start = (f32[8,112,256]{2,1,0:T(8,128)S(1)}, f32[8,112,256]{2,1,0:T(8,128)S(1)}, u32[]{:S(2)}, u32[]{:S(2)}) collective-permute-start(f32[8,112,256]{2,1,0:T(8,128)S(1)} %get-tuple-element.19), channel_id=1, source_target_pairs={{0,1},{1,0},{2,3},{3,2},{4,5},{5,4},{6,7},{7,6},{8,9},{9,8},{10,11... | collective-permute-start | bytes 2752520 | tf_op jit(solution)/shard_map/ppermute | solution.py:508
  14.4 0.6 copy-start.4
  15.1 0.7 copy-start.8
  15.7 0.6 copy-start.9
  16.4 0.7 copy-start.10
  17.0 6.4 %collective-permute-start.1 = (f32[112,256]{1,0:T(8,128)S(1)}, f32[112,256]{1,0:T(8,128)S(1)}, u32[]{:S(2)}, u32[]{:S(2)}) collective-permute-start(f32[112,256]{1,0:T(8,128)S(1)} %get-tuple-element.21), channel_id=1, source_target_pairs={{0,2},{2,0},{4,6},{6,4},{8,10},{10,8},{12,14},{14,12},{16,18},{18,... | collective-permute-start | bytes 344072 | tf_op jit(solution)/shard_map/ppermute | solution.py:504
  19.9 7.7 %collective-permute-start.2 = (f32[112,256]{1,0:T(8,128)}, f32[112,256]{1,0:T(8,128)}, u32[]{:S(2)}, u32[]{:S(2)}) collective-permute-start(f32[112,256]{1,0:T(8,128)} %get-tuple-element.22), channel_id=1, source_target_pairs={{0,4},{2,6},{4,0},{6,2},{8,12},{10,14},{12,8},{14,10},{16,20},{18,... | collective-permute-start | bytes 344072 | tf_op jit(solution)/shard_map/ppermute | solution.py:504
  21.4 6.8 %collective-permute-start.3 = (f32[112,256]{1,0:T(8,128)}, f32[112,256]{1,0:T(8,128)}, u32[]{:S(2)}, u32[]{:S(2)}) collective-permute-start(f32[112,256]{1,0:T(8,128)} %get-tuple-element.23), channel_id=1, source_target_pairs={{0,6},{2,4},{4,2},{6,0},{8,14},{10,12},{12,10},{14,8},{16,22},{18,... | collective-permute-start | bytes 344072 | tf_op jit(solution)/shard_map/ppermute | solution.py:504
  21.4 9.1 %collective-permute-start.4 = (f32[112,256]{1,0:T(8,128)}, f32[112,256]{1,0:T(8,128)}, u32[]{:S(2)}, u32[]{:S(2)}) collective-permute-start(f32[112,256]{1,0:T(8,128)} %get-tuple-element.24), channel_id=1, source_target_pairs={{0,8},{2,10},{4,12},{6,14},{8,0},{10,2},{12,4},{14,6},{16,24},{18,... | collective-permute-start | bytes 344072 | tf_op jit(solution)/shard_map/ppermute | solution.py:504
  23.4 0.6 copy-start.6
  24.1 29.1 %collective-permute-start.18 = (f32[7,128,128]{2,1,0:T(8,128)}, f32[7,128,128]{2,1,0:T(8,128)}, u32[]{:S(2)}, u32[]{:S(2)}) collective-permute-start(f32[7,128,128]{2,1,0:T(8,128)} %q_hbm.5), channel_id=1, source_target_pairs={{0,1},{1,0},{2,3},{3,2},{4,5},{5,4},{6,7},{7,6},{8,9},{9,8},{10,11... | collective-permute-start | bytes 1376264 | tf_op jit(solution)/shard_map/ppermute | solution.py:508
  27.5 6.8 %collective-permute-start.5 = (f32[112,256]{1,0:T(8,128)}, f32[112,256]{1,0:T(8,128)S(1)}, u32[]{:S(2)}, u32[]{:S(2)}) collective-permute-start(f32[112,256]{1,0:T(8,128)} %copy-done.10), channel_id=1, source_target_pairs={{0,10},{2,8},{4,14},{6,12},{8,2},{10,0},{12,6},{14,4},{16,26},{18,... | collective-permute-start | bytes 344072 | tf_op jit(solution)/shard_map/ppermute | solution.py:504
  28.2 8.4 %collective-permute-start.6 = (f32[112,256]{1,0:T(8,128)}, f32[112,256]{1,0:T(8,128)S(1)}, u32[]{:S(2)}, u32[]{:S(2)}) collective-permute-start(f32[112,256]{1,0:T(8,128)} %copy-done.9), channel_id=1, source_target_pairs={{0,12},{2,14},{4,8},{6,10},{8,4},{10,6},{12,0},{14,2},{16,28},{18,... | collective-permute-start | bytes 344072 | tf_op jit(solution)/shard_map/ppermute | solution.py:504
  30.5 8.1 %collective-permute-start.7 = (f32[112,256]{1,0:T(8,128)}, f32[112,256]{1,0:T(8,128)S(1)}, u32[]{:S(2)}, u32[]{:S(2)}) collective-permute-start(f32[112,256]{1,0:T(8,128)} %copy-done.8), channel_id=1, source_target_pairs={{0,14},{2,12},{4,10},{6,8},{8,6},{10,4},{12,2},{14,0},{16,30},{18,... | collective-permute-start | bytes 344072 | tf_op jit(solution)/shard_map/ppermute | solution.py:504
  34.4 9.7 %collective-permute-start.9 = (f32[112,256]{1,0:T(8,128)S(1)}, f32[112,256]{1,0:T(8,128)S(1)}, u32[]{:S(2)}, u32[]{:S(2)}) collective-permute-start(f32[112,256]{1,0:T(8,128)S(1)} %constant_dynamic-slice_fusion), channel_id=1, source_target_pairs={{0,1},{1,0},{2,3},{3,2},{4,5},{5,4},{6,7},{7,6},{8,9},{9,8},{10,11... | collective-permute-start | bytes 344072 | tf_op jit(solution)/shard_map/ppermute | solution.py:508
  38.6 0.9 %copy-start.5 = (f32[112,256]{1,0:T(8,128)S(1)}, f32[112,256]{1,0:T(8,128)}, u32[]{:S(2)}) copy-start(f32[112,256]{1,0:T(8,128)} %copy-done.4) | copy-start | bytes 344068
  39.5 0.9 %copy-start.7 = (f32[112,256]{1,0:T(8,128)S(1)}, f32[112,256]{1,0:T(8,128)}, u32[]{:S(2)}) copy-start(f32[112,256]{1,0:T(8,128)} %copy-done.6) | copy-start | bytes 344068
  41.4 7.0 %collective-permute-start.8 = (f32[112,256]{1,0:T(8,128)S(1)}, f32[112,256]{1,0:T(8,128)S(1)}, u32[]{:S(2)}, u32[]{:S(2)}) collective-permute-start(f32[112,256]{1,0:T(8,128)S(1)} %sum_slots.1.refs_0_), channel_id=1, source_target_pairs={{0,16},{2,18},{4,20},{6,22},{8,24},{10,26},{12,28},{14,30},{16,0},... | collective-permute-start | bytes 344072 | tf_op jit(solution)/shard_map/ppermute | solution.py:504
  48.4 1.0 %copy-start.2 = (f32[7,128,128]{2,1,0:T(8,128)S(1)}, f32[7,128,128]{2,1,0:T(8,128)}, u32[]{:S(2)}) copy-start(f32[7,128,128]{2,1,0:T(8,128)} %copy-done.1) | copy-start | bytes 1376260
  49.6 17.4 %copy-start.3 = (f32[7,128,128]{2,1,0:T(8,128)S(1)}, f32[7,128,128]{2,1,0:T(8,128)}, u32[]{:S(2)}) copy-start(f32[7,128,128]{2,1,0:T(8,128)} %copy-done.1) | copy-start | bytes 1376260
  49.6 6.1 %collective-permute-start.10 = (f32[112,256]{1,0:T(8,128)S(1)}, f32[112,256]{1,0:T(8,128)S(1)}, u32[]{:S(2)}, u32[]{:S(2)}) collective-permute-start(f32[112,256]{1,0:T(8,128)S(1)} %side_slot.1.refs_0_), channel_id=1, source_target_pairs={{0,2},{2,0},{4,6},{6,4},{8,10},{10,8},{12,14},{14,12},{16,18},{18,... | collective-permute-start | bytes 344072 | tf_op jit(solution)/shard_map/ppermute | solution.py:504
  50.4 8.5 %collective-permute-start.11 = (f32[112,256]{1,0:T(8,128)S(1)}, f32[112,256]{1,0:T(8,128)S(1)}, u32[]{:S(2)}, u32[]{:S(2)}) collective-permute-start(f32[112,256]{1,0:T(8,128)S(1)} %side_slot.1.refs_0_), channel_id=1, source_target_pairs={{0,4},{2,6},{4,0},{6,2},{8,12},{10,14},{12,8},{14,10},{16,20},{18,... | collective-permute-start | bytes 344072 | tf_op jit(solution)/shard_map/ppermute | solution.py:504
  51.4 13.0 %collective-permute-start.12 = (f32[112,256]{1,0:T(8,128)S(1)}, f32[112,256]{1,0:T(8,128)S(1)}, u32[]{:S(2)}, u32[]{:S(2)}) collective-permute-start(f32[112,256]{1,0:T(8,128)S(1)} %side_slot.1.refs_0_), channel_id=1, source_target_pairs={{0,6},{2,4},{4,2},{6,0},{8,14},{10,12},{12,10},{14,8},{16,22},{18,... | collective-permute-start | bytes 344072 | tf_op jit(solution)/shard_map/ppermute | solution.py:504
  53.2 11.2 %collective-permute-start.13 = (f32[112,256]{1,0:T(8,128)S(1)}, f32[112,256]{1,0:T(8,128)S(1)}, u32[]{:S(2)}, u32[]{:S(2)}) collective-permute-start(f32[112,256]{1,0:T(8,128)S(1)} %side_slot.1.refs_0_), channel_id=1, source_target_pairs={{0,8},{2,10},{4,12},{6,14},{8,0},{10,2},{12,4},{14,6},{16,24},{18,... | collective-permute-start | bytes 344072 | tf_op jit(solution)/shard_map/ppermute | solution.py:504
  55.7 8.7 %collective-permute-start.14 = (f32[112,256]{1,0:T(8,128)S(1)}, f32[112,256]{1,0:T(8,128)S(1)}, u32[]{:S(2)}, u32[]{:S(2)}) collective-permute-start(f32[112,256]{1,0:T(8,128)S(1)} %side_slot.1.refs_0_), channel_id=1, source_target_pairs={{0,10},{2,8},{4,14},{6,12},{8,2},{10,0},{12,6},{14,4},{16,26},{18,... | collective-permute-start | bytes 344072 | tf_op jit(solution)/shard_map/ppermute | solution.py:504
  58.9 5.7 %collective-permute-start.15 = (f32[112,256]{1,0:T(8,128)S(1)}, f32[112,256]{1,0:T(8,128)S(1)}, u32[]{:S(2)}, u32[]{:S(2)}) collective-permute-start(f32[112,256]{1,0:T(8,128)S(1)} %side_slot.1.refs_0_), channel_id=1, source_target_pairs={{0,12},{2,14},{4,8},{6,10},{8,4},{10,6},{12,0},{14,2},{16,28},{18,... | collective-permute-start | bytes 344072 | tf_op jit(solution)/shard_map/ppermute | solution.py:504
  58.9 7.7 %collective-permute-start.16 = (f32[112,256]{1,0:T(8,128)S(1)}, f32[112,256]{1,0:T(8,128)S(1)}, u32[]{:S(2)}, u32[]{:S(2)}) collective-permute-start(f32[112,256]{1,0:T(8,128)S(1)} %side_slot.1.refs_0_), channel_id=1, source_target_pairs={{0,14},{2,12},{4,10},{6,8},{8,6},{10,4},{12,2},{14,0},{16,30},{18,... | collective-permute-start | bytes 344072 | tf_op jit(solution)/shard_map/ppermute | solution.py:504
  70.7 8.3 %collective-permute-start.19 = (f32[896,256]{1,0:T(8,128)S(1)}, f32[896,256]{1,0:T(8,128)S(1)}, u32[]{:S(2)}, u32[]{:S(2)}) collective-permute-start(f32[896,256]{1,0:T(8,128)S(1)} %get-tuple-element.31), channel_id=1, source_target_pairs={{0,1},{1,0},{2,3},{3,2},{4,5},{5,4},{6,7},{7,6},{8,9},{9,8},{10,11... | collective-permute-start | bytes 2752520 | tf_op jit(solution)/shard_map/ppermute | solution.py:508
